TPU v7x, 32 devices: a whole 2x2x4 slice. The times are simulated.
32 devices in a mesh: row: 4 (over z), col: 8 (over y, x, core).
Axes of the slice: x: 2, y: 2, z: 4, core: 2. Of those that a mesh axis runs over, the one named last changes fastest.
Arguments:
- panel_block: float32 [512, 512], P(('row', 'col')), may hold values from -1 to 10, as said below
- panel_cross: float32 [8192, 512], P('col'), may hold values from -0.375 to 0.375
- trail_block: float32 [8192, 8192], P('row', 'col'), may hold values from -1.2 to 1.2
- panel_pixels: float32 [512, 16384], P('row', 'col'), may hold values from -0.375 to 0.375
- trail_pixels: float32 [8192, 16384], P('row', 'col'), may hold values from -1.2 to 1.2
- panel_sectors: float32 [512, 1024], P('row'), may hold values from -6 to 6
- trail_sectors: float32 [8192, 1024], P('col', 'row'), may hold values from -1.2 to 1.2
Outputs:
- panel_factor: float32 [512, 512], P(('row', 'col'))
- panel_columns: float32 [8192, 512], P('col')
- trail_updated: float32 [8192, 8192], P('row', 'col')
- pixels_updated: float32 [8192, 16384], P('row', 'col')
- sectors_updated: float32 [8192, 1024], P('col', 'row')
- prediction: float32 [16384, 1024], P('col', 'row')
Inputs may be any that keep to these rules, and one draw needn't show every extreme that they name: `panel_block`: symmetric positive definite.
All inputs are finite; a program needn't handle non-finite values.
Results may differ from a plain program's by a relative error of at most 0.000075.
Values sent between devices are 32-bit elements; how exact they have to be, the bound alone decides.
No kernel may reach another device: no remote copies, remote signals or barrier semaphores. Data moves between devices by JAX's collectives and lax.ppermute only.
A program may use at most 128 MiB of HBM per device.

v0:
```python
import jax
import jax.numpy as jnp
from jax import lax
from jax.experimental import pallas as pl
from jax.experimental.pallas import tpu as pltpu
from jax.sharding import PartitionSpec as P


HIGHEST = lax.Precision.HIGHEST
LANES = 128
SUBLANES = 8
COLUMN_STEPS = 4


def invert_block(tiles):
    count = len(tiles)
    width = tiles[0].shape[1]
    shape = (SUBLANES, width)
    lane = lax.broadcasted_iota(jnp.int32, shape, 1)
    sub = lax.broadcasted_iota(jnp.int32, shape, 0)

    def lanes_of(x, j):
        return jnp.broadcast_to(x[:, j : j + 1], shape)

    def row_of(x, i):
        return jnp.broadcast_to(x[i : i + 1, :], shape)

    m = list(tiles)
    out = []
    for g in range(count):
        base = SUBLANES * g
        inside = (lane >= base) & (lane < base + SUBLANES)
        columns = [[lanes_of(m[v], base + q) for q in range(SUBLANES)] for v in range(g, count)]
        s = [
            [row_of(columns[0][q], i) if i >= q else None for q in range(SUBLANES)]
            for i in range(SUBLANES)
        ]
        low = [[None] * SUBLANES for _ in range(SUBLANES)]
        pivot_inv = []
        root_inv = []
        for q in range(SUBLANES):
            pivot_inv.append(1.0 / s[q][q])
            root_inv.append(lax.rsqrt(s[q][q]))
            for i in range(q + 1, SUBLANES):
                low[i][q] = s[i][q] * pivot_inv[q]
            for i in range(q + 1, SUBLANES):
                for k in range(q + 1, i + 1):
                    s[i][k] = s[i][k] - low[i][q] * s[k][q]
        rows = []
        for q in range(SUBLANES):
            x = jnp.where(inside, jnp.where(lane == base + q, 1.0, 0.0), row_of(m[g], q))
            for p in range(q):
                x = x - low[q][p] * rows[p]
            rows.append(x)
        own = jnp.zeros(shape, jnp.float32)
        for q in range(SUBLANES):
            own = jnp.where((sub == q) & (lane <= base + q), rows[q] * root_inv[q], own)
        out.append(own)
        for v in range(g + 1, count):
            done = []
            for q in range(SUBLANES):
                x = columns[v - g][q]
                for p in range(q):
                    x = x - done[p] * low[q][p]
                done.append(x)
            x = jnp.where(inside, 0.0, m[v])
            for q in range(SUBLANES):
                x = x - (done[q] * pivot_inv[q]) * rows[q]
            m[v] = x
    return out


def factor_step(k, m_ref, l_ref, wk_ref):
    size = m_ref.shape[0]
    width = wk_ref.shape[0]
    offset = k * width if isinstance(k, int) else pl.multiple_of(k * width, width)
    span = pl.ds(offset, width)
    block = m_ref.at[span, span]
    tiles = [block[i : i + SUBLANES, :] for i in range(0, width, SUBLANES)]
    for i, tile in enumerate(invert_block(tiles)):
        wk_ref[i * SUBLANES : (i + 1) * SUBLANES, :] = tile
    inverse = wk_ref[...]
    panel = lax.dot_general(
        m_ref[:, span],
        inverse,
        (((1,), (1,)), ((), ())),
        precision=HIGHEST,
        preferred_element_type=jnp.float32,
    )
    row = lax.broadcasted_iota(jnp.int32, (size, width), 0)
    col = lax.broadcasted_iota(jnp.int32, (size, width), 1) + offset
    below = row >= offset + width
    l_ref[:, span] = jnp.where(row >= col, panel, 0.0)
    ii = lax.broadcasted_iota(jnp.int32, (width, width), 0)
    jj = lax.broadcasted_iota(jnp.int32, (width, width), 1)
    m_ref[span, span] = jnp.where(ii == jj, 1.0, 0.0)
    upper = jnp.dot(inverse, m_ref[span, :], precision=HIGHEST, preferred_element_type=jnp.float32)
    lane = lax.broadcasted_iota(jnp.int32, (width, size), 1)
    m_ref[:, span] = jnp.where(below, 0.0, m_ref[:, span])
    m_ref[...] = m_ref[...] - jnp.dot(
        jnp.where(below, panel, 0.0),
        upper,
        precision=HIGHEST,
        preferred_element_type=jnp.float32,
    )
    m_ref[span, :] = jnp.where(lane < offset + width, upper, 0.0)


def first_kernel(place_ref, *refs):
    pieces, (l_ref, m_ref, wk_ref) = refs[:-3], refs[-3:]
    n_row, count, _ = pieces[0].shape
    for t, piece in enumerate(pieces):
        for m in range(n_row):
            slot = (place_ref[0] ^ m) * len(pieces) + (place_ref[1] ^ t)
            m_ref[pl.ds(pl.multiple_of(slot * count, count), count), :] = piece[m]
    l_ref[...] = jnp.zeros_like(l_ref)

    @pl.loop(0, m_ref.shape[0] // wk_ref.shape[0] // 2)
    def _(k):
        factor_step(k, m_ref, l_ref, wk_ref)


def second_kernel(l_in, m_in, l_ref, m_ref, wk_ref):
    l_ref[...] = l_in[...]
    m_ref[...] = m_in[...]
    blocks = m_ref.shape[0] // wk_ref.shape[0]

    @pl.loop(blocks // 2, blocks - 1)
    def _(k):
        factor_step(k, m_ref, l_ref, wk_ref)


def third_kernel(place_ref, l_in, m_in, c_ref, *refs):
    results, refs = refs[:6], refs[6:]
    stores, (l_ref, m_ref, wk_ref, sems) = refs[:6], refs[6:]
    rows_out, o_ref, oh, ol, wh, wl = stores
    l_ref[...] = l_in[...]
    m_ref[...] = m_in[...]
    blocks = m_ref.shape[0] // wk_ref.shape[0]

    factor_step(blocks - 1, m_ref, l_ref, wk_ref)
    count = rows_out.shape[0]
    if count == l_ref.shape[0]:
        rows_out[...] = l_ref[...]
    else:
        rows_out[...] = l_ref[pl.ds(pl.multiple_of(place_ref[0] * count, count), count), :]
    wh[...], wl[...] = split(m_ref[...])
    copies = []

    def send(i, span):
        copy = pltpu.make_async_copy(
            stores[i].at[span], results[i].at[span], sems.at[len(copies)]
        )
        copy.start()
        copies.append(copy)

    for i in (0, 4, 5):
        send(i, pl.ds(0, stores[i].shape[0]))
    step = c_ref.shape[0] // COLUMN_STEPS
    for t in range(COLUMN_STEPS):
        span = pl.ds(t * step, step)
        out = lower_nt(split(c_ref[span, :]), (wh, wl))
        o_ref[span, :] = out
        oh[span, :], ol[span, :] = split(out)
        for i in (1, 2, 3):
            send(i, span)
    for copy in copies:
        copy.wait()


def factor_parts(size):
    square = shape(size, size)
    scratch = [pltpu.VMEM((LANES, LANES), jnp.float32)]
    vmem = pl.BlockSpec(memory_space=pltpu.VMEM)
    smem = pl.BlockSpec(memory_space=pltpu.SMEM)

    def first(place, pieces):
        return pl.pallas_call(
            first_kernel,
            out_shape=(square, square),
            in_specs=[smem] + [vmem] * len(pieces),
            out_specs=(vmem, vmem),
            scratch_shapes=scratch,
            name="factor_first",
        )(place, *pieces)

    def second(low, m):
        return pl.pallas_call(
            second_kernel,
            out_shape=(square, square),
            in_specs=[vmem, vmem],
            out_specs=(vmem, vmem),
            scratch_shapes=scratch,
            name="factor_second",
        )(low, m)

    def third(place, low, m, cross, count):
        rows = cross.shape[0]
        results = (
            (shape(count, size), shape(rows, size))
            + pair_shape(rows, size)
            + pair_shape(size, size)
        )
        return pl.pallas_call(
            third_kernel,
            out_shape=results,
            in_specs=[smem, vmem, vmem, vmem],
            out_specs=(pl.BlockSpec(memory_space=pltpu.HBM),) * len(results),
            scratch_shapes=[pltpu.VMEM(x.shape, x.dtype) for x in results]
            + [pltpu.VMEM((size, size), jnp.float32)] * 2
            + scratch
            + [pltpu.SemaphoreType.DMA((3 + 3 * COLUMN_STEPS,))],
            name="factor_third",
        )(place, low, m, cross)

    return first, second, third


NT = ((1,), (1,))
NN = ((1,), (0,))
TN = ((0,), (0,))


def split(x):
    high = x.astype(jnp.bfloat16)
    return high, (x - high.astype(jnp.float32)).astype(jnp.bfloat16)


def product(a, b, dims):
    def one(x, y):
        return lax.dot_general(x, y, (dims, ((), ())), preferred_element_type=jnp.float32)

    return one(a[0], b[0]) + (one(a[0], b[1]) + one(a[1], b[0]))


def shape(*dims, dtype=jnp.float32):
    return jax.ShapeDtypeStruct(dims, dtype)


def pair_shape(*dims):
    return (shape(*dims, dtype=jnp.bfloat16),) * 2


def in_hbm(x):
    return pltpu.with_memory_space_constraint(x, pltpu.HBM)


def full(*dims):
    return pl.BlockSpec(dims, lambda i, *_: (0,) * len(dims))


def tiles(*dims):
    return pl.BlockSpec(dims, lambda i, *_: (i,) + (0,) * (len(dims) - 1))


def run(kernel, grid, in_specs, out_specs, out_shape, scratch=(), prefetch=0, alias={}):
    return pl.pallas_call(
        kernel,
        grid_spec=pltpu.PrefetchScalarGridSpec(
            num_scalar_prefetch=prefetch,
            grid=(grid,),
            in_specs=in_specs,
            out_specs=out_specs,
            scratch_shapes=list(scratch),
        ),
        out_shape=out_shape,
        input_output_aliases=alias,
        compiler_params=pltpu.CompilerParams(vmem_limit_bytes=48 << 20),
    )


def lower_nt(x, w_refs):
    pw = w_refs[0].shape[0]
    h = pw // 2
    top = product((x[0][:, :h], x[1][:, :h]), tuple(w[:h, :h] for w in w_refs), NT)
    low = product(x, tuple(w[h:, :] for w in w_refs), NT)
    return jnp.concatenate([top, low], 1)


def lower_nn(x, w_refs):
    pw = w_refs[0].shape[0]
    h = pw // 2
    left = product(x, tuple(w[:, :h] for w in w_refs), NN)
    right = product((x[0][:, h:], x[1][:, h:]), tuple(w[h:, h:] for w in w_refs), NN)
    return jnp.concatenate([left, right], 1)


def placed(flag_ref, masks, refs, out_refs):
    for m, x in zip(masks, refs):
        if isinstance(x, tuple):
            value = jnp.where(flag_ref[2] != 0, x[0][...], x[1][...])
        else:
            value = x[...]
        size = value.shape[0]
        span = pl.ds(pl.multiple_of((flag_ref[0] ^ m) * size, size), size)
        for out, part in zip(out_refs, split(value)):
            out[span, :] = part


def rows(picks, crosses, inverse, own, trail, tile):
    count, pw = crosses[0].shape
    total, width = trail.shape
    steps = count // tile

    def kernel(pick_ref, *refs):
        choices, (wh, wl, oh, ol, t_ref, out_ref, ch_ref, cl_ref) = (
            refs[: len(crosses)],
            refs[len(crosses) :],
        )
        pick = pick_ref[pl.program_id(0) // steps]
        x = choices[0][...]
        for i in range(1, len(choices)):
            x = jnp.where(pick == i, choices[i][...], x)
        r = split(lower_nt(split(x), (wh, wl)))
        out_ref[...] = t_ref[...] - product(r, (oh[...], ol[...]), NT)
        ch_ref[...], cl_ref[...] = split(lower_nn(r, (wh, wl)))

    side = pl.BlockSpec((tile, pw), lambda i, p: (i % steps, 0))
    return run(
        kernel,
        total // tile,
        [side] * len(crosses)
        + [full(pw, pw)] * 2
        + [full(*own[0].shape)] * 2
        + [tiles(tile, width)],
        (tiles(tile, width), tiles(tile, pw), tiles(tile, pw)),
        (shape(total, width),) + (pltpu.HBM((total, pw), jnp.bfloat16),) * 2,
        prefetch=1,
    )(picks, *crosses, *inverse, *own, trail)


def flatten(pieces):
    return [x for p in pieces for x in (p if isinstance(p, tuple) else (p,))]


def regroup(pieces, refs):
    it = iter(refs)
    return [(next(it), next(it)) if isinstance(p, tuple) else next(it) for p in pieces]


def maps(flags, masks, pieces, sectors, inverse, own, coupling, base, trail, tile):
    total, width = base.shape
    arrays = flatten(pieces)
    pw = inverse[0].shape[0]
    steps = total // tile
    own_rows, own_width = trail.shape
    own_tile, cut = own_rows // steps, width // steps
    n, k = len(arrays), len(sectors)

    def kernel(flag_ref, *refs):
        parts, sector_parts, refs = refs[:n], refs[n : n + k], refs[n + k :]
        wh, wl, oh, ol, ch, cl, b_ref, t_ref = refs[:8]
        out_ref, sec_ref, pred_ref, ph, plow, sh, sl, kh, kl = refs[8:]
        i = pl.program_id(0)

        @pl.when(i == 0)
        def _():
            placed(flag_ref, masks, regroup(pieces, parts), (ph, plow))
            placed(flag_ref, masks, sector_parts, (sh, sl))
            pair = (wh[...], wl[...])
            solved = split(product(pair, (sh[...], sl[...]), NN))
            sh[...], sl[...] = solved
            kh[...], kl[...] = split(product(pair, solved, TN))

        out_ref[...] = b_ref[...] - product((ch[...], cl[...]), (ph[...], plow[...]), NN)
        sec_ref[...] = t_ref[...] - product((oh[...], ol[...]), (sh[...], sl[...]), NN)
        span = pl.ds(pl.multiple_of(i * cut, cut), cut)
        pred_ref[...] = product((ph[:, span], plow[:, span]), (kh[...], kl[...]), TN)

    return run(
        kernel,
        steps,
        [full(*x.shape) for x in arrays + list(sectors)]
        + [full(pw, pw)] * 2
        + [tiles(own_tile, pw)] * 2
        + [tiles(tile, pw)] * 2
        + [tiles(tile, width), tiles(own_tile, own_width)],
        (tiles(tile, width), tiles(own_tile, own_width), tiles(cut, own_width)),
        (shape(total, width), shape(own_rows, own_width), shape(width, own_width)),
        scratch=[pltpu.VMEM((pw, width), jnp.bfloat16)] * 2
        + [pltpu.VMEM((pw, own_width), jnp.bfloat16)] * 4,
        prefetch=1,
    )(flags, *arrays, *sectors, *inverse, *own, *coupling, base, trail)


def exchange(x, axis, size, mask):
    return lax.ppermute(x, axis, [(i, i ^ mask) for i in range(size)])


def update(
    panel_block, panel_cross, trail_block, panel_pixels, trail_pixels, panel_sectors, trail_sectors
):
    n_row = lax.axis_size("row")
    n_col = lax.axis_size("col")
    r = lax.axis_index("row")
    c = lax.axis_index("col")
    count, pw = panel_block.shape
    owners = n_col // n_row
    first, second, third = factor_parts(pw)
    forward = n_row == 4
    masks = [0, 2, 1, 3] if forward else list(range(n_row))

    stack = [panel_block] + [exchange(panel_block, "row", n_row, m) for m in range(1, n_row)]
    stack = jnp.stack(stack)
    even = [stack] + [exchange(stack, "col", n_col, m) for m in range(2, n_col, 2)]
    odd = [exchange(x, "col", n_col, 1) for x in even]
    pieces = [x for pair in zip(even, odd) for x in pair]
    if count % SUBLANES:
        whole = jnp.stack(pieces)[jnp.arange(n_col) ^ c][:, jnp.arange(n_row) ^ r]
        whole = whole.transpose(1, 0, 2, 3).reshape(1, 1, pw, pw)
        pieces = [whole[0]]
        place = jnp.zeros((2,), jnp.int32)
    else:
        place = jnp.stack([r, c]).astype(jnp.int32)

    width = panel_sectors.shape[1] // n_row
    cut = lambda m: lax.dynamic_slice_in_dim(panel_sectors, (r ^ m) * width, width, 1)
    sector_pieces = [exchange(cut(m), "row", n_row, m) if m else cut(m) for m in masks]
    if forward:
        two = exchange(panel_pixels, "row", n_row, 2)
        near = exchange(panel_pixels, "row", n_row, 1)
        middle = lax.ppermute(panel_pixels, "row", [(1, 2), (2, 1)])
    else:
        pixel_pieces = [
            exchange(panel_pixels, "row", n_row, m) if m else panel_pixels for m in masks
        ]

    low, m = first(place, pieces)
    bits = n_col.bit_length() - 1
    parity = c % 2
    held = panel_cross
    orders = [[1 + (s + j) % (bits - 1) for s in range(bits - 1)] for j in range(owners)]
    reached = [[0] for _ in range(owners)]
    early = bits == 3
    for s in range(bits - 1):
        pairs = []
        receives = jnp.zeros((), jnp.bool_)
        for j in range(owners):
            bit = 1 << orders[j][s]
            for i in range(n_row):
                base = i * owners + j
                pairs += [(i * n_col + (base ^ x), i * n_col + (base ^ x ^ bit)) for x in reached[j]]
            for x in reached[j]:
                receives |= c == ((r * owners + j) ^ x ^ bit)
            reached[j] += [x ^ bit for x in reached[j]]
        got = lax.ppermute(held, ("row", "col"), pairs)
        if early and s == bits - 2:
            break
        held = jnp.where(receives, got, held)
    if early:
        beside = exchange(held, "col", n_col, 1)
        last = exchange(got, "col", n_col, 1)
        seat = c ^ (r * owners)
        source = seat < 2
        holder = source | (seat == (1 << orders[0][0])) | (seat == ((1 << orders[1][0]) | 1))
        mate = (seat == ((1 << orders[0][0]) | 1)) | (seat == (1 << orders[1][0]))
        crosses = [held, beside, got, last]
        kept = jnp.where(holder, 0, 2)
        swapped = jnp.where(source, 1, jnp.where(mate, 1, 3))
    else:
        crosses = [held, exchange(held, "col", n_col, 1)]
        kept, swapped = 0 * c, 0 * c + 1
    ints = lambda *v: jnp.stack([jnp.asarray(x, jnp.int32) for x in v])
    picks = ints(
        jnp.where(parity == 0, kept, swapped),
        jnp.where(parity == 0, swapped, kept),
    )

    whole_rows = count % SUBLANES != 0
    low, m = second(low, m)
    if forward:
        far = lax.ppermute(two, "row", [(1, 0), (2, 3)])
        pixel_pieces = [panel_pixels, two, near, (middle, far)]
    factor_rows, column_own, *pairs = third(
        ints(r * n_col + c), low, m, panel_cross, pw if whole_rows else count
    )
    pairs = [in_hbm(x) for x in pairs]
    own, inverse = pairs[0:2], pairs[2:4]
    if whole_rows:
        factor_rows = lax.dynamic_slice_in_dim(factor_rows, (r * n_col + c) * count, count, 0)
    tile = min(512, panel_cross.shape[0])
    trail_updated, *coupling = rows(picks, crosses, inverse, own, trail_block, tile)
    coupling = [in_hbm(x) for x in coupling]
    flags = ints(r, 0, (r == 1) | (r == 2))
    pixel_total, sectors_updated, predicted = maps(
        flags, masks, pixel_pieces, sector_pieces, inverse, own, coupling,
        trail_pixels, trail_sectors, tile,
    )
    return (factor_rows, column_own, trail_updated, pixel_total, sectors_updated, predicted)


def solution(mesh):
    return jax.shard_map(
        update,
        mesh=mesh,
        in_specs=(
            P(("row", "col"), None),
            P("col", None),
            P("row", "col"),
            P("row", "col"),
            P("row", "col"),
            P("row", None),
            P("col", "row"),
        ),
        out_specs=(
            P(("row", "col"), None),
            P("col", None),
            P("row", "col"),
            P("row", "col"),
            P("col", "row"),
            P("col", "row"),
        ),
        check_vma=False,
    )
```

profile of v0, /device:TPU:19, one launch (start us, length us, event | category | flops | bytes accessed | tf_op | source)
XLA Modules:
  0.0 214.7 jit_solution(2007639858810488104)
XLA Ops:
  0.6 2.0 collective-permute-start.10
  2.6 2.2 %broadcast_select_fusion.refs_0_ = f32[1024,512]{1,0:T(8,128)S(1)} fusion(f32[1024,512]{1,0:T(8,128)} %collective-permute-done.10, f32[1024,512]{1,0:T(8,128)} %c_ref.1, pred[]{:T(512)S(6)} %or.18), kind=kLoop, calls=%fused_computation | loop fusion | flops 524288 | bytes 6291457 | tf_op jit(solution)/shard_map/jit(_where)/select_n | solution.py:449
  4.8 1.3 collective-permute-start.12
  6.1 0.7 collective-permute-start.11
  6.9 48.3 %collective-permute-done.12.refs_2_ = f32[1024,512]{1,0:T(8,128)} collective-permute-done((f32[1024,512]{1,0:T(8,128)S(1)}, f32[1024,512]{1,0:T(8,128)}, u32[]{:S(2)}, u32[]{:S(2)}) %collective-permute-start.12) | collective-permute-done | bytes 2097184 | tf_op jit(solution)/shard_map/ppermute | solution.py:446
  55.2 3.4 %collective-permute-start.13 = (f32[1024,512]{1,0:T(8,128)}, f32[1024,512]{1,0:T(8,128)}, u32[]{:S(2)}, u32[]{:S(2)}) collective-permute-start(f32[1024,512]{1,0:T(8,128)} %collective-permute-done.12.refs_2_), channel_id=1, source_target_pairs={{0,1},{1,0},{2,3},{3,2},{4,5},{5,4},{6,7},{7,6},{8,9},{9,8},{10,11... | collective-permute-start | bytes 6291464 | tf_op jit(solution)/shard_map/ppermute | solution.py:387
  58.6 2.6 %collective-permute-start.2 = (f32[16,512]{1,0:T(8,128)S(1)}, f32[16,512]{1,0:T(8,128)S(1)}, u32[]{:S(2)}, u32[]{:S(2)}) collective-permute-start(f32[16,512]{1,0:T(8,128)S(1)} %copy-done.9), channel_id=1, source_target_pairs={{0,24},{8,16},{16,8},{24,0},{1,25},{9,17},{17,9},{25,1},{2,26},{10... | collective-permute-start | bytes 98312 | tf_op jit(solution)/shard_map/ppermute | solution.py:387
  61.2 21.1 %collective-permute-done = f32[16,512]{1,0:T(8,128)S(1)} collective-permute-done((f32[16,512]{1,0:T(8,128)S(1)}, f32[16,512]{1,0:T(8,128)S(1)}, u32[]{:S(2)}, u32[]{:S(2)}) %collective-permute-start) | collective-permute-done | bytes 32800 | tf_op jit(solution)/shard_map/ppermute | solution.py:387
  82.3 1.9 collective-permute-start.1
  84.2 1.8 constant_dynamic-slice_fusion
  86.0 23.5 %collective-permute-done.2 = f32[16,512]{1,0:T(8,128)S(1)} collective-permute-done((f32[16,512]{1,0:T(8,128)S(1)}, f32[16,512]{1,0:T(8,128)S(1)}, u32[]{:S(2)}, u32[]{:S(2)}) %collective-permute-start.2) | collective-permute-done | bytes 32800 | tf_op jit(solution)/shard_map/ppermute | solution.py:387
  109.5 0.7 collective-permute-start.20
  110.3 3.0 %collective-permute-done.20.refs_8_ = f32[128,256]{1,0:T(8,128)S(1)} collective-permute-done((f32[128,256]{1,0:T(8,128)S(1)}, f32[128,256]{1,0:T(8,128)S(1)}, u32[]{:S(2)}, u32[]{:S(2)}) %collective-permute-start.20) | collective-permute-done | bytes 131104 | tf_op jit(solution)/shard_map/ppermute | solution.py:387
  113.3 2.1 collective-permute-done.8.refs_6_
  115.4 1.4 collective-permute-start.4
  116.8 1.0 collective-permute-done.6.refs_4_
  117.8 3.1 %collective-permute-start.3 = (f32[4,16,512]{2,1,0:T(8,128)S(1)}, f32[4,16,512]{2,1,0:T(8,128)S(1)}, u32[]{:S(2)}, u32[]{:S(2)}) collective-permute-start(f32[4,16,512]{2,1,0:T(8,128)S(1)} %pad_maximum_fusion.refs_0_), channel_id=1, source_target_pairs={{0,1},{1,0},{2,3},{3,2},{4,5},{5,4},{6,7},{7,6},{8,9},{9,8},{10,11... | collective-permute-start | bytes 393224 | tf_op jit(solution)/shard_map/ppermute | solution.py:387
  120.9 1.2 collective-permute-start.9
  122.1 0.1 collective-permute-start.7
  122.3 0.8 collective-permute-done.9.refs_7_
  123.1 0.4 collective-permute-start.5
  123.5 1.3 collective-permute-start.15
  124.8 3.2 %collective-permute-start.16 = (f32[128,2048]{1,0:T(8,128)S(1)}, f32[128,2048]{1,0:T(8,128)}, u32[]{:S(2)}, u32[]{:S(2)}) collective-permute-start(f32[128,2048]{1,0:T(8,128)S(1)} %copy-done), channel_id=1, source_target_pairs={{8,16},{16,8},{9,17},{17,9},{10,18},{18,10},{11,19},{19,11},{12,20... | collective-permute-start | bytes 3145736 | tf_op jit(solution)/shard_map/ppermute | solution.py:422
  128.1 2.3 %collective-permute-start.17 = (f32[128,2048]{1,0:T(8,128)}, f32[128,2048]{1,0:T(8,128)}, u32[]{:S(2)}, u32[]{:S(2)}) collective-permute-start(f32[128,2048]{1,0:T(8,128)} %collective-permute-done.14.refs_1_), channel_id=1, source_target_pairs={{8,0},{16,24},{9,1},{17,25},{10,2},{18,26},{11,3},{19,27},{12,4},{... | collective-permute-start | bytes 3145736 | tf_op jit(solution)/shard_map/ppermute | solution.py:472
  130.5 2.0 collective-permute-start.19
  132.4 0.6 pad_add_fusion.place_ref
  133.0 0.1 pad_add_fusion.2.flag_ref
  133.1 14.9 %factor_first.1 = (f32[512,512]{1,0:T(8,128)}, f32[512,512]{1,0:T(8,128)}) custom-call(s32[2]{0:T(128)} %pad_add_fusion.place_ref, f32[4,16,512]{2,1,0:T(8,128)} %copy-done.1, f32[4,16,512]{2,1,0:T(8,128)} %copy-done.5, f32[4,16,512]{2,1,0:T(8,128)} %copy-done.4, f32[4,16,512]{2,1,0:T(8,128)} %copy-done.8, f32[4,16,512]{2,1,0:T(8,128)} %copy-done.3, ...), custom_call_target="tpu_custom_call" | custom-call | tf_op jit(solution)/shard_map/factor_first/pallas_call | solution.py:178
  148.0 8.9 %factor_second.1 = (f32[512,512]{1,0:T(8,128)}, f32[512,512]{1,0:T(8,128)}) custom-call(f32[512,512]{1,0:T(8,128)} %get-tuple-element.22.l_in, f32[512,512]{1,0:T(8,128)} %get-tuple-element.23.m_in), custom_call_target="tpu_custom_call" | custom-call | tf_op jit(solution)/shard_map/factor_second/pallas_call | solution.py:188
  156.9 11.1 %factor_third.1 = (f32[16,512]{1,0:T(8,128)}, f32[1024,512]{1,0:T(8,128)}, bf16[1024,512]{1,0:T(8,128)(2,1)}, bf16[1024,512]{1,0:T(8,128)(2,1)}, bf16[512,512]{1,0:T(8,128)(2,1)}, /*index=5*/bf16[512,512]{1,0:T(8,128)(2,1)}) custom-call(s32[1]{0:T(128)} %bitcast.place_ref, f32[512,512]{1,0:T(8,128)} %get-tuple-element.24.l_in, ...), custom_call_target="tpu_custom_call" | custom-call | tf_op jit(solution)/shard_map/factor_third/pallas_call | solution.py:204
  168.0 19.5 %shard_map.118 = (f32[2048,1024]{1,0:T(8,128)}, bf16[2048,512]{1,0:T(8,128)(2,1)}, bf16[2048,512]{1,0:T(8,128)(2,1)}) custom-call(s32[2]{0:T(128)S(1)} %pad_add_fusion.1.pick_ref, f32[1024,512]{1,0:T(8,128)S(1)} %broadcast_select_fusion.refs_0_, f32[1024,512]{1,0:T(8,128)} %collective-permute-done.11.refs_1_, f32[1024,512]{1,0:T(8,128)} %collective-permute-done.12.refs_2_, ...), custom_call_target="tpu_custom_call" | custom-call | tf_op jit(solution)/shard_map/pallas_call | solution.py:319
  187.6 27.0 %shard_map.119 = (f32[2048,2048]{1,0:T(8,128)}, f32[1024,256]{1,0:T(8,128)}, f32[2048,256]{1,0:T(8,128)}) custom-call(s32[3]{0:T(128)S(1)} %pad_add_fusion.2.flag_ref, f32[128,2048]{1,0:T(8,128)S(1)} %copy-done, f32[128,2048]{1,0:T(8,128)} %collective-permute-done.14.refs_1_, f32[128,2048]{1,0:T(8,128)} %collective-permute-done.15.refs_2_, ...), custom_call_target="tpu_custom_call" | custom-call | tf_op jit(solution)/shard_map/pallas_call | solution.py:370
  (41 shorter events, 0.3 us)
Async XLA Ops:
  0.6 2.0 collective-permute-start.10
  2.6 55.9 %copy-start = (f32[128,2048]{1,0:T(8,128)S(1)}, f32[128,2048]{1,0:T(8,128)}, u32[]{:S(2)}) copy-start(f32[128,2048]{1,0:T(8,128)} %refs_0_.1) | copy-start | bytes 3145732
  2.6 55.9 %copy-start.9 = (f32[16,512]{1,0:T(8,128)S(1)}, f32[16,512]{1,0:T(8,128)}, u32[]{:S(2)}) copy-start(f32[16,512]{1,0:T(8,128)} %param.7) | copy-start | bytes 98308
  4.8 50.3 %collective-permute-start.12 = (f32[1024,512]{1,0:T(8,128)S(1)}, f32[1024,512]{1,0:T(8,128)}, u32[]{:S(2)}, u32[]{:S(2)}) collective-permute-start(f32[1024,512]{1,0:T(8,128)S(1)} %broadcast_select_fusion.refs_0_), channel_id=1, source_target_pairs={{0,4},{2,6},{10,14},{8,12},{20,16},{22,18},{30,26},{28,24},{1,3},{... | collective-permute-start | bytes 6291464 | tf_op jit(solution)/shard_map/ppermute | solution.py:446
  6.1 124.3 %collective-permute-start.11 = (f32[1024,512]{1,0:T(8,128)S(1)}, f32[1024,512]{1,0:T(8,128)}, u32[]{:S(2)}, u32[]{:S(2)}) collective-permute-start(f32[1024,512]{1,0:T(8,128)S(1)} %broadcast_select_fusion.refs_0_), channel_id=1, source_target_pairs={{0,1},{1,0},{2,3},{3,2},{4,5},{5,4},{6,7},{7,6},{8,9},{9,8},{10,11... | collective-permute-start | bytes 6291464 | tf_op jit(solution)/shard_map/ppermute | solution.py:387
  55.2 75.3 %collective-permute-start.13 = (f32[1024,512]{1,0:T(8,128)}, f32[1024,512]{1,0:T(8,128)}, u32[]{:S(2)}, u32[]{:S(2)}) collective-permute-start(f32[1024,512]{1,0:T(8,128)} %collective-permute-done.12.refs_2_), channel_id=1, source_target_pairs={{0,1},{1,0},{2,3},{3,2},{4,5},{5,4},{6,7},{7,6},{8,9},{9,8},{10,11... | collective-permute-start | bytes 6291464 | tf_op jit(solution)/shard_map/ppermute | solution.py:387
  58.5 69.4 %collective-permute-start.14 = (f32[128,2048]{1,0:T(8,128)S(1)}, f32[128,2048]{1,0:T(8,128)}, u32[]{:S(2)}, u32[]{:S(2)}) collective-permute-start(f32[128,2048]{1,0:T(8,128)S(1)} %copy-done), channel_id=1, source_target_pairs={{0,16},{8,24},{16,0},{24,8},{1,17},{9,25},{17,1},{25,9},{2,18},{10... | collective-permute-start | bytes 3145736 | tf_op jit(solution)/shard_map/ppermute | solution.py:387
  58.6 23.7 %collective-permute-start = (f32[16,512]{1,0:T(8,128)S(1)}, f32[16,512]{1,0:T(8,128)S(1)}, u32[]{:S(2)}, u32[]{:S(2)}) collective-permute-start(f32[16,512]{1,0:T(8,128)S(1)} %copy-done.9), channel_id=1, source_target_pairs={{0,8},{8,0},{16,24},{24,16},{1,9},{9,1},{17,25},{25,17},{2,10},{10... | collective-permute-start | bytes 98312 | tf_op jit(solution)/shard_map/ppermute | solution.py:387
  58.6 50.8 %collective-permute-start.2 = (f32[16,512]{1,0:T(8,128)S(1)}, f32[16,512]{1,0:T(8,128)S(1)}, u32[]{:S(2)}, u32[]{:S(2)}) collective-permute-start(f32[16,512]{1,0:T(8,128)S(1)} %copy-done.9), channel_id=1, source_target_pairs={{0,24},{8,16},{16,8},{24,0},{1,25},{9,17},{17,9},{25,1},{2,26},{10... | collective-permute-start | bytes 98312 | tf_op jit(solution)/shard_map/ppermute | solution.py:387
  82.3 27.9 %collective-permute-start.1 = (f32[16,512]{1,0:T(8,128)S(1)}, f32[16,512]{1,0:T(8,128)S(1)}, u32[]{:S(2)}, u32[]{:S(2)}) collective-permute-start(f32[16,512]{1,0:T(8,128)S(1)} %copy-done.9), channel_id=1, source_target_pairs={{0,16},{8,24},{16,0},{24,8},{1,17},{9,25},{17,1},{25,9},{2,18},{10... | collective-permute-start | bytes 98312 | tf_op jit(solution)/shard_map/ppermute | solution.py:387
  109.5 3.8 %collective-permute-start.20 = (f32[128,256]{1,0:T(8,128)S(1)}, f32[128,256]{1,0:T(8,128)S(1)}, u32[]{:S(2)}, u32[]{:S(2)}) collective-permute-start(f32[128,256]{1,0:T(8,128)S(1)} %get-tuple-element.38), channel_id=1, source_target_pairs={{0,24},{8,16},{16,8},{24,0},{1,25},{9,17},{17,9},{25,1},{2,26},{10... | collective-permute-start | bytes 393224 | tf_op jit(solution)/shard_map/ppermute | solution.py:387
  110.2 17.8 %copy-start.1 = (f32[4,16,512]{2,1,0:T(8,128)}, f32[4,16,512]{2,1,0:T(8,128)S(1)}, u32[]{:S(2)}) copy-start(f32[4,16,512]{2,1,0:T(8,128)S(1)} %pad_maximum_fusion.refs_0_) | copy-start | bytes 393220
  110.2 5.2 %collective-permute-start.8 = (f32[4,16,512]{2,1,0:T(8,128)S(1)}, f32[4,16,512]{2,1,0:T(8,128)S(1)}, u32[]{:S(2)}, u32[]{:S(2)}) collective-permute-start(f32[4,16,512]{2,1,0:T(8,128)S(1)} %pad_maximum_fusion.refs_0_), channel_id=1, source_target_pairs={{0,6},{1,7},{2,4},{3,5},{4,2},{5,3},{6,0},{7,1},{8,14},{9,15},{10,... | collective-permute-start | bytes 393224 | tf_op jit(solution)/shard_map/ppermute | solution.py:387
  113.3 4.5 %collective-permute-start.6 = (f32[4,16,512]{2,1,0:T(8,128)S(1)}, f32[4,16,512]{2,1,0:T(8,128)S(1)}, u32[]{:S(2)}, u32[]{:S(2)}) collective-permute-start(f32[4,16,512]{2,1,0:T(8,128)S(1)} %pad_maximum_fusion.refs_0_), channel_id=1, source_target_pairs={{0,4},{1,5},{2,6},{3,7},{4,0},{5,1},{6,2},{7,3},{8,12},{9,13},{10,... | collective-permute-start | bytes 393224 | tf_op jit(solution)/shard_map/ppermute | solution.py:387
  115.4 12.6 %copy-start.2 = (f32[4,16,512]{2,1,0:T(8,128)}, f32[4,16,512]{2,1,0:T(8,128)S(1)}, u32[]{:S(2)}) copy-start(f32[4,16,512]{2,1,0:T(8,128)S(1)} %collective-permute-done.8.refs_6_) | copy-start | bytes 393220
  115.4 5.5 %collective-permute-start.4 = (f32[4,16,512]{2,1,0:T(8,128)S(1)}, f32[4,16,512]{2,1,0:T(8,128)S(1)}, u32[]{:S(2)}, u32[]{:S(2)}) collective-permute-start(f32[4,16,512]{2,1,0:T(8,128)S(1)} %pad_maximum_fusion.refs_0_), channel_id=1, source_target_pairs={{0,2},{1,3},{2,0},{3,1},{4,6},{5,7},{6,4},{7,5},{8,10},{9,11},{10,... | collective-permute-start | bytes 393224 | tf_op jit(solution)/shard_map/ppermute | solution.py:387
  117.8 10.2 %copy-start.3 = (f32[4,16,512]{2,1,0:T(8,128)}, f32[4,16,512]{2,1,0:T(8,128)S(1)}, u32[]{:S(2)}) copy-start(f32[4,16,512]{2,1,0:T(8,128)S(1)} %collective-permute-done.6.refs_4_) | copy-start | bytes 393220
  117.8 4.3 %collective-permute-start.3 = (f32[4,16,512]{2,1,0:T(8,128)S(1)}, f32[4,16,512]{2,1,0:T(8,128)S(1)}, u32[]{:S(2)}, u32[]{:S(2)}) collective-permute-start(f32[4,16,512]{2,1,0:T(8,128)S(1)} %pad_maximum_fusion.refs_0_), channel_id=1, source_target_pairs={{0,1},{1,0},{2,3},{3,2},{4,5},{5,4},{6,7},{7,6},{8,9},{9,8},{10,11... | collective-permute-start | bytes 393224 | tf_op jit(solution)/shard_map/ppermute | solution.py:387
  120.9 7.1 %copy-start.4 = (f32[4,16,512]{2,1,0:T(8,128)}, f32[4,16,512]{2,1,0:T(8,128)S(1)}, u32[]{:S(2)}) copy-start(f32[4,16,512]{2,1,0:T(8,128)S(1)} %collective-permute-done.4.refs_2_) | copy-start | bytes 393220
  120.9 2.2 %collective-permute-start.9 = (f32[4,16,512]{2,1,0:T(8,128)S(1)}, f32[4,16,512]{2,1,0:T(8,128)S(1)}, u32[]{:S(2)}, u32[]{:S(2)}) collective-permute-start(f32[4,16,512]{2,1,0:T(8,128)S(1)} %collective-permute-done.8.refs_6_), channel_id=1, source_target_pairs={{0,1},{1,0},{2,3},{3,2},{4,5},{5,4},{6,7},{7,6},{8,9},{9,8},{10,11... | collective-permute-start | bytes 393224 | tf_op jit(solution)/shard_map/ppermute | solution.py:387
  122.1 5.9 %copy-start.5 = (f32[4,16,512]{2,1,0:T(8,128)}, f32[4,16,512]{2,1,0:T(8,128)S(1)}, u32[]{:S(2)}) copy-start(f32[4,16,512]{2,1,0:T(8,128)S(1)} %collective-permute-done.3.refs_1_) | copy-start | bytes 393220
  122.1 1.3 collective-permute-start.7
  123.1 4.9 %copy-start.6 = (f32[4,16,512]{2,1,0:T(8,128)}, f32[4,16,512]{2,1,0:T(8,128)S(1)}, u32[]{:S(2)}) copy-start(f32[4,16,512]{2,1,0:T(8,128)S(1)} %collective-permute-done.9.refs_7_) | copy-start | bytes 393220
  123.1 1.7 collective-permute-start.5
  123.5 4.6 %copy-start.7 = (f32[4,16,512]{2,1,0:T(8,128)}, f32[4,16,512]{2,1,0:T(8,128)S(1)}, u32[]{:S(2)}) copy-start(f32[4,16,512]{2,1,0:T(8,128)S(1)} %collective-permute-done.7.refs_5_) | copy-start | bytes 393220
  123.5 64.1 %collective-permute-start.15 = (f32[128,2048]{1,0:T(8,128)S(1)}, f32[128,2048]{1,0:T(8,128)}, u32[]{:S(2)}, u32[]{:S(2)}) collective-permute-start(f32[128,2048]{1,0:T(8,128)S(1)} %copy-done), channel_id=1, source_target_pairs={{0,8},{8,0},{16,24},{24,16},{1,9},{9,1},{17,25},{25,17},{2,10},{10... | collective-permute-start | bytes 3145736 | tf_op jit(solution)/shard_map/ppermute | solution.py:387
  124.8 3.3 %copy-start.8 = (f32[4,16,512]{2,1,0:T(8,128)}, f32[4,16,512]{2,1,0:T(8,128)S(1)}, u32[]{:S(2)}) copy-start(f32[4,16,512]{2,1,0:T(8,128)S(1)} %collective-permute-done.5.refs_3_) | copy-start | bytes 393220
  124.8 62.8 %collective-permute-start.16 = (f32[128,2048]{1,0:T(8,128)S(1)}, f32[128,2048]{1,0:T(8,128)}, u32[]{:S(2)}, u32[]{:S(2)}) collective-permute-start(f32[128,2048]{1,0:T(8,128)S(1)} %copy-done), channel_id=1, source_target_pairs={{8,16},{16,8},{9,17},{17,9},{10,18},{18,10},{11,19},{19,11},{12,20... | collective-permute-start | bytes 3145736 | tf_op jit(solution)/shard_map/ppermute | solution.py:422
  128.1 59.5 %collective-permute-start.17 = (f32[128,2048]{1,0:T(8,128)}, f32[128,2048]{1,0:T(8,128)}, u32[]{:S(2)}, u32[]{:S(2)}) collective-permute-start(f32[128,2048]{1,0:T(8,128)} %collective-permute-done.14.refs_1_), channel_id=1, source_target_pairs={{8,0},{16,24},{9,1},{17,25},{10,2},{18,26},{11,3},{19,27},{12,4},{... | collective-permute-start | bytes 3145736 | tf_op jit(solution)/shard_map/ppermute | solution.py:472
  130.5 57.1 %collective-permute-start.18 = (f32[128,256]{1,0:T(8,128)}, f32[128,256]{1,0:T(8,128)S(1)}, u32[]{:S(2)}, u32[]{:S(2)}) collective-permute-start(f32[128,256]{1,0:T(8,128)} %get-tuple-element.39), channel_id=1, source_target_pairs={{0,16},{8,24},{16,0},{24,8},{1,17},{9,25},{17,1},{25,9},{2,18},{10... | collective-permute-start | bytes 393224 | tf_op jit(solution)/shard_map/ppermute | solution.py:387
  130.5 57.1 %collective-permute-start.19 = (f32[128,256]{1,0:T(8,128)}, f32[128,256]{1,0:T(8,128)}, u32[]{:S(2)}, u32[]{:S(2)}) collective-permute-start(f32[128,256]{1,0:T(8,128)} %get-tuple-element.41), channel_id=1, source_target_pairs={{0,8},{8,0},{16,24},{24,16},{1,9},{9,1},{17,25},{25,17},{2,10},{10... | collective-permute-start | bytes 393224 | tf_op jit(solution)/shard_map/ppermute | solution.py:387
where the time goes:
time: 218 us; the launch traced here: 215 us
  waiting for transfers between devices  99.8 us (46%)
  Pallas kernels  81.4 us (37%)
  starting transfers between devices  27.7 us (13%)
  other arithmetic  2.91 us (1%)
    ppermute x17, waiting for transfers between devices, exchange(): return lax.ppermute(x, axis, [(i, i ^ mask) for i in range(size)])  51.5 us
    ppermute x2, waiting for transfers between devices, update(): got = lax.ppermute(held, ('row', 'col'), pairs)  48.3 us
    pallas_call x1, Pallas kernels, maps(): run(kernel, steps, [full(*x.shape) for x in arrays + list(sectors)] + [fu...  27 us
    pallas_call x1, Pallas kernels, rows(): run(kernel, total // tile, [side] * len(crosses) + [full(pw, pw)] * 2 + [...  19.5 us
    ppermute x17, starting transfers between devices, exchange(): return lax.ppermute(x, axis, [(i, i ^ mask) for i in range(size)])  18.9 us
    pallas_call x1, Pallas kernels, first(): pl.pallas_call(first_kernel, out_shape=(square, square), in_specs=[smem]...  14.9 us
    pallas_call x1, Pallas kernels, third(): pl.pallas_call(third_kernel, out_shape=results, in_specs=[smem, vmem, vme...  11.1 us
    pallas_call x1, Pallas kernels, second(): pl.pallas_call(second_kernel, out_shape=(square, square), in_specs=[vmem,...  8.88 us
  transfers between devices with their start and end apart: 21, of which 7 were waited for; matrix products, arithmetic and copies ran while one was open for 1% of the time, Pallas kernels for 25%

commit v1 on v0

--- a/solution.py
+++ b/solution.py
@@ -9,7 +9,6 @@
 HIGHEST = lax.Precision.HIGHEST
 LANES = 128
 SUBLANES = 8
-COLUMN_STEPS = 4
 
 
 def invert_block(tiles):
@@ -80,29 +79,34 @@
     for i, tile in enumerate(invert_block(tiles)):
         wk_ref[i * SUBLANES : (i + 1) * SUBLANES, :] = tile
     inverse = wk_ref[...]
+    start = offset if isinstance(k, int) else 0
     panel = lax.dot_general(
-        m_ref[:, span],
+        m_ref[start:, span],
         inverse,
         (((1,), (1,)), ((), ())),
         precision=HIGHEST,
         preferred_element_type=jnp.float32,
     )
-    row = lax.broadcasted_iota(jnp.int32, (size, width), 0)
-    col = lax.broadcasted_iota(jnp.int32, (size, width), 1) + offset
+    row = lax.broadcasted_iota(jnp.int32, (size - start, width), 0) + start
+    col = lax.broadcasted_iota(jnp.int32, (size - start, width), 1) + offset
     below = row >= offset + width
-    l_ref[:, span] = jnp.where(row >= col, panel, 0.0)
+    l_ref[start:, span] = jnp.where(row >= col, panel, 0.0)
     ii = lax.broadcasted_iota(jnp.int32, (width, width), 0)
     jj = lax.broadcasted_iota(jnp.int32, (width, width), 1)
     m_ref[span, span] = jnp.where(ii == jj, 1.0, 0.0)
     upper = jnp.dot(inverse, m_ref[span, :], precision=HIGHEST, preferred_element_type=jnp.float32)
     lane = lax.broadcasted_iota(jnp.int32, (width, size), 1)
-    m_ref[:, span] = jnp.where(below, 0.0, m_ref[:, span])
-    m_ref[...] = m_ref[...] - jnp.dot(
-        jnp.where(below, panel, 0.0),
-        upper,
-        precision=HIGHEST,
-        preferred_element_type=jnp.float32,
-    )
+    if isinstance(k, int):
+        start += width
+        panel = panel[width:, :]
+        m_ref[:, span] = jnp.zeros((size, width), jnp.float32)
+    else:
+        m_ref[:, span] = jnp.where(below, 0.0, m_ref[:, span])
+        panel = jnp.where(below, panel, 0.0)
+    if start < size:
+        m_ref[start:, :] = m_ref[start:, :] - jnp.dot(
+            panel, upper, precision=HIGHEST, preferred_element_type=jnp.float32
+        )
     m_ref[span, :] = jnp.where(lane < offset + width, upper, 0.0)
 
 
@@ -125,45 +129,27 @@
     m_ref[...] = m_in[...]
     blocks = m_ref.shape[0] // wk_ref.shape[0]
 
-    @pl.loop(blocks // 2, blocks - 1)
-    def _(k):
+    for k in range(blocks // 2, blocks - 1):
         factor_step(k, m_ref, l_ref, wk_ref)
 
 
-def third_kernel(place_ref, l_in, m_in, c_ref, *refs):
-    results, refs = refs[:6], refs[6:]
-    stores, (l_ref, m_ref, wk_ref, sems) = refs[:6], refs[6:]
-    rows_out, o_ref, oh, ol, wh, wl = stores
+def third_kernel(place_ref, l_in, m_in, *refs):
+    results, (rows_out, wh, wl), (l_ref, m_ref, wk_ref, sems) = refs[:3], refs[3:6], refs[6:]
     l_ref[...] = l_in[...]
     m_ref[...] = m_in[...]
-    blocks = m_ref.shape[0] // wk_ref.shape[0]
-
-    factor_step(blocks - 1, m_ref, l_ref, wk_ref)
+    factor_step(m_ref.shape[0] // wk_ref.shape[0] - 1, m_ref, l_ref, wk_ref)
     count = rows_out.shape[0]
     if count == l_ref.shape[0]:
         rows_out[...] = l_ref[...]
     else:
         rows_out[...] = l_ref[pl.ds(pl.multiple_of(place_ref[0] * count, count), count), :]
     wh[...], wl[...] = split(m_ref[...])
-    copies = []
-
-    def send(i, span):
-        copy = pltpu.make_async_copy(
-            stores[i].at[span], results[i].at[span], sems.at[len(copies)]
-        )
+    copies = [
+        pltpu.make_async_copy(x, y, sems.at[i])
+        for i, (x, y) in enumerate(zip((rows_out, wh, wl), results))
+    ]
+    for copy in copies:
         copy.start()
-        copies.append(copy)
-
-    for i in (0, 4, 5):
-        send(i, pl.ds(0, stores[i].shape[0]))
-    step = c_ref.shape[0] // COLUMN_STEPS
-    for t in range(COLUMN_STEPS):
-        span = pl.ds(t * step, step)
-        out = lower_nt(split(c_ref[span, :]), (wh, wl))
-        o_ref[span, :] = out
-        oh[span, :], ol[span, :] = split(out)
-        for i in (1, 2, 3):
-            send(i, span)
     for copy in copies:
         copy.wait()
 
@@ -194,24 +180,19 @@
             name="factor_second",
         )(low, m)
 
-    def third(place, low, m, cross, count):
-        rows = cross.shape[0]
-        results = (
-            (shape(count, size), shape(rows, size))
-            + pair_shape(rows, size)
-            + pair_shape(size, size)
-        )
+    def third(place, low, m, count):
+        results = (shape(count, size),) + pair_shape(size, size)
         return pl.pallas_call(
             third_kernel,
             out_shape=results,
-            in_specs=[smem, vmem, vmem, vmem],
+            in_specs=[smem, vmem, vmem],
             out_specs=(pl.BlockSpec(memory_space=pltpu.HBM),) * len(results),
             scratch_shapes=[pltpu.VMEM(x.shape, x.dtype) for x in results]
             + [pltpu.VMEM((size, size), jnp.float32)] * 2
             + scratch
-            + [pltpu.SemaphoreType.DMA((3 + 3 * COLUMN_STEPS,))],
+            + [pltpu.SemaphoreType.DMA((len(results),))],
             name="factor_third",
-        )(place, low, m, cross)
+        )(place, low, m)
 
     return first, second, third
 
@@ -269,6 +250,23 @@
     )
 
 
+def columns(cross, inverse, tile):
+    count, pw = cross.shape
+
+    def kernel(c_ref, wh, wl, o_ref, oh_ref, ol_ref):
+        out = lower_nt(split(c_ref[...]), (wh, wl))
+        o_ref[...] = out
+        oh_ref[...], ol_ref[...] = split(out)
+
+    return run(
+        kernel,
+        count // tile,
+        [tiles(tile, pw)] + [full(pw, pw)] * 2,
+        (tiles(tile, pw),) * 3,
+        (shape(count, pw),) + (pltpu.HBM((count, pw), jnp.bfloat16),) * 2,
+    )(cross, *inverse)
+
+
 def lower_nt(x, w_refs):
     pw = w_refs[0].shape[0]
     h = pw // 2
@@ -315,11 +313,15 @@
         out_ref[...] = t_ref[...] - product(r, (oh[...], ol[...]), NT)
         ch_ref[...], cl_ref[...] = split(lower_nn(r, (wh, wl)))
 
-    side = pl.BlockSpec((tile, pw), lambda i, p: (i % steps, 0))
+    def side(which):
+        return pl.BlockSpec(
+            (tile, pw), lambda i, p: (jnp.where(p[i // steps] == which, i % steps, 0), 0)
+        )
+
     return run(
         kernel,
         total // tile,
-        [side] * len(crosses)
+        [side(k) for k in range(len(crosses))]
         + [full(pw, pw)] * 2
         + [full(*own[0].shape)] * 2
         + [tiles(tile, width)],
@@ -414,11 +416,13 @@
         place = jnp.stack([r, c]).astype(jnp.int32)
 
     width = panel_sectors.shape[1] // n_row
-    cut = lambda m: lax.dynamic_slice_in_dim(panel_sectors, (r ^ m) * width, width, 1)
-    sector_pieces = [exchange(cut(m), "row", n_row, m) if m else cut(m) for m in masks]
+    cuts = [
+        lax.dynamic_slice_in_dim(panel_sectors, (r ^ m) * width, width, 1) for m in masks
+    ]
+    sector_pieces = [exchange(x, "row", n_row, m) if m else x for x, m in zip(cuts, masks)]
     if forward:
+        near = exchange(panel_pixels, "row", n_row, 1)
         two = exchange(panel_pixels, "row", n_row, 2)
-        near = exchange(panel_pixels, "row", n_row, 1)
         middle = lax.ppermute(panel_pixels, "row", [(1, 2), (2, 1)])
     else:
         pixel_pieces = [
@@ -471,11 +475,10 @@
     if forward:
         far = lax.ppermute(two, "row", [(1, 0), (2, 3)])
         pixel_pieces = [panel_pixels, two, near, (middle, far)]
-    factor_rows, column_own, *pairs = third(
-        ints(r * n_col + c), low, m, panel_cross, pw if whole_rows else count
-    )
-    pairs = [in_hbm(x) for x in pairs]
-    own, inverse = pairs[0:2], pairs[2:4]
+    factor_rows, *inverse = third(ints(r * n_col + c), low, m, pw if whole_rows else count)
+    inverse = [in_hbm(x) for x in inverse]
+    column_own, *own = columns(panel_cross, inverse, min(256, panel_cross.shape[0]))
+    own = [in_hbm(x) for x in own]
     if whole_rows:
         factor_rows = lax.dynamic_slice_in_dim(factor_rows, (r * n_col + c) * count, count, 0)
     tile = min(512, panel_cross.shape[0])

time: 218 us -> 219 us (level)
    pallas_call x1 -> x2, Pallas kernels: 19.5 us -> 24.1 us  [the longest x1 19.2 us: rows(): run(kernel, total // tile, [side(k) for k in range(len(crosses))] + [full...]
    pallas_call x1, Pallas kernels: 11.1 us -> 7.56 us  [third(): pl.pallas_call(third_kernel, out_shape=results, in_specs=[smem, vmem, vme...]
where the time goes in v1:
time: 219 us; the launch traced here: 216 us
  waiting for transfers between devices  99.8 us (46%)
  Pallas kernels  82.2 us (38%)
  starting transfers between devices  27.8 us (13%)
  other arithmetic  2.99 us (1%)
    ppermute x17, waiting for transfers between devices, exchange(): return lax.ppermute(x, axis, [(i, i ^ mask) for i in range(size)])  51.5 us
    ppermute x2, waiting for transfers between devices, update(): got = lax.ppermute(held, ('row', 'col'), pairs)  48.3 us
    pallas_call x1, Pallas kernels, maps(): run(kernel, steps, [full(*x.shape) for x in arrays + list(sectors)] + [fu...  27.2 us
    pallas_call x1, Pallas kernels, rows(): run(kernel, total // tile, [side(k) for k in range(len(crosses))] + [full...  19.2 us
    ppermute x17, starting transfers between devices, exchange(): return lax.ppermute(x, axis, [(i, i ^ mask) for i in range(size)])  18.9 us
    pallas_call x1, Pallas kernels, first(): pl.pallas_call(first_kernel, out_shape=(square, square), in_specs=[smem]...  14.9 us
    pallas_call x1, Pallas kernels, second(): pl.pallas_call(second_kernel, out_shape=(square, square), in_specs=[vmem,...  8.38 us
    pallas_call x1, Pallas kernels, third(): pl.pallas_call(third_kernel, out_shape=results, in_specs=[smem, vmem, vme...  7.56 us
  transfers between devices with their start and end apart: 21, of which 7 were waited for; matrix products, arithmetic and copies ran while one was open for 1% of the time, Pallas kernels for 25%

profile of v1, /device:TPU:19, one launch (start us, length us, event | category | flops | bytes accessed | tf_op | source)
XLA Modules:
  0.0 215.7 jit_solution(7659066556148569251)
XLA Ops:
  0.6 2.0 collective-permute-start.10
  2.7 2.2 %broadcast_select_fusion.refs_0_ = f32[1024,512]{1,0:T(8,128)S(1)} fusion(f32[1024,512]{1,0:T(8,128)} %collective-permute-done.10, f32[1024,512]{1,0:T(8,128)} %c_ref.1, pred[]{:T(512)S(6)} %or.18), kind=kLoop, calls=%fused_computation | loop fusion | flops 524288 | bytes 6291457 | tf_op jit(solution)/shard_map/jit(_where)/select_n | solution.py:453
  4.8 1.3 collective-permute-start.12
  6.1 0.7 collective-permute-start.11
  6.9 48.3 %collective-permute-done.12.refs_2_ = f32[1024,512]{1,0:T(8,128)} collective-permute-done((f32[1024,512]{1,0:T(8,128)S(1)}, f32[1024,512]{1,0:T(8,128)}, u32[]{:S(2)}, u32[]{:S(2)}) %collective-permute-start.12) | collective-permute-done | bytes 2097184 | tf_op jit(solution)/shard_map/ppermute | solution.py:450
  55.2 3.4 %collective-permute-start.13 = (f32[1024,512]{1,0:T(8,128)}, f32[1024,512]{1,0:T(8,128)}, u32[]{:S(2)}, u32[]{:S(2)}) collective-permute-start(f32[1024,512]{1,0:T(8,128)} %collective-permute-done.12.refs_2_), channel_id=1, source_target_pairs={{0,1},{1,0},{2,3},{3,2},{4,5},{5,4},{6,7},{7,6},{8,9},{9,8},{10,11... | collective-permute-start | bytes 6291464 | tf_op jit(solution)/shard_map/ppermute | solution.py:389
  58.6 2.6 %collective-permute-start.2 = (f32[16,512]{1,0:T(8,128)S(1)}, f32[16,512]{1,0:T(8,128)S(1)}, u32[]{:S(2)}, u32[]{:S(2)}) collective-permute-start(f32[16,512]{1,0:T(8,128)S(1)} %copy-done.12), channel_id=1, source_target_pairs={{0,24},{8,16},{16,8},{24,0},{1,25},{9,17},{17,9},{25,1},{2,26},{10... | collective-permute-start | bytes 98312 | tf_op jit(solution)/shard_map/ppermute | solution.py:389
  61.2 21.1 %collective-permute-done = f32[16,512]{1,0:T(8,128)S(1)} collective-permute-done((f32[16,512]{1,0:T(8,128)S(1)}, f32[16,512]{1,0:T(8,128)S(1)}, u32[]{:S(2)}, u32[]{:S(2)}) %collective-permute-start) | collective-permute-done | bytes 32800 | tf_op jit(solution)/shard_map/ppermute | solution.py:389
  82.3 1.9 collective-permute-start.1
  84.2 1.8 constant_dynamic-slice_fusion
  86.0 23.5 %collective-permute-done.2 = f32[16,512]{1,0:T(8,128)S(1)} collective-permute-done((f32[16,512]{1,0:T(8,128)S(1)}, f32[16,512]{1,0:T(8,128)S(1)}, u32[]{:S(2)}, u32[]{:S(2)}) %collective-permute-start.2) | collective-permute-done | bytes 32800 | tf_op jit(solution)/shard_map/ppermute | solution.py:389
  109.5 0.7 collective-permute-start.20
  110.3 3.0 %collective-permute-done.20.refs_8_ = f32[128,256]{1,0:T(8,128)S(1)} collective-permute-done((f32[128,256]{1,0:T(8,128)S(1)}, f32[128,256]{1,0:T(8,128)S(1)}, u32[]{:S(2)}, u32[]{:S(2)}) %collective-permute-start.20) | collective-permute-done | bytes 131104 | tf_op jit(solution)/shard_map/ppermute | solution.py:389
  113.3 2.1 collective-permute-done.8.refs_6_
  115.4 1.4 collective-permute-start.4
  116.8 1.0 collective-permute-done.6.refs_4_
  117.8 3.1 %collective-permute-start.3 = (f32[4,16,512]{2,1,0:T(8,128)S(1)}, f32[4,16,512]{2,1,0:T(8,128)S(1)}, u32[]{:S(2)}, u32[]{:S(2)}) collective-permute-start(f32[4,16,512]{2,1,0:T(8,128)S(1)} %pad_maximum_fusion.refs_0_), channel_id=1, source_target_pairs={{0,1},{1,0},{2,3},{3,2},{4,5},{5,4},{6,7},{7,6},{8,9},{9,8},{10,11... | collective-permute-start | bytes 393224 | tf_op jit(solution)/shard_map/ppermute | solution.py:389
  120.9 1.2 collective-permute-start.9
  122.1 0.1 collective-permute-start.7
  122.3 0.8 collective-permute-done.9.refs_7_
  123.1 0.4 collective-permute-start.5
  123.5 1.3 collective-permute-start.15
  124.8 3.2 %collective-permute-start.16 = (f32[128,2048]{1,0:T(8,128)S(1)}, f32[128,2048]{1,0:T(8,128)}, u32[]{:S(2)}, u32[]{:S(2)}) collective-permute-start(f32[128,2048]{1,0:T(8,128)S(1)} %copy-done.3), channel_id=1, source_target_pairs={{8,16},{16,8},{9,17},{17,9},{10,18},{18,10},{11,19},{19,11},{12,20... | collective-permute-start | bytes 3145736 | tf_op jit(solution)/shard_map/ppermute | solution.py:426
  128.1 2.3 %collective-permute-start.17 = (f32[128,2048]{1,0:T(8,128)}, f32[128,2048]{1,0:T(8,128)}, u32[]{:S(2)}, u32[]{:S(2)}) collective-permute-start(f32[128,2048]{1,0:T(8,128)} %collective-permute-done.14.refs_1_), channel_id=1, source_target_pairs={{8,0},{16,24},{9,1},{17,25},{10,2},{18,26},{11,3},{19,27},{12,4},{... | collective-permute-start | bytes 3145736 | tf_op jit(solution)/shard_map/ppermute | solution.py:476
  130.5 2.0 collective-permute-start.19
  132.5 0.7 pad_add_fusion.place_ref
  133.2 14.9 %factor_first.1 = (f32[512,512]{1,0:T(8,128)}, f32[512,512]{1,0:T(8,128)}) custom-call(s32[2]{0:T(128)} %pad_add_fusion.place_ref, f32[4,16,512]{2,1,0:T(8,128)} %copy-done.4, f32[4,16,512]{2,1,0:T(8,128)} %copy-done.8, f32[4,16,512]{2,1,0:T(8,128)} %copy-done.7, f32[4,16,512]{2,1,0:T(8,128)} %copy-done.11, f32[4,16,512]{2,1,0:T(8,128)} %copy-done.6, ...), custom_call_target="tpu_custom_call" | custom-call | tf_op jit(solution)/shard_map/factor_first/pallas_call | solution.py:164
  148.1 8.4 %factor_second.1 = (f32[512,512]{1,0:T(8,128)}, f32[512,512]{1,0:T(8,128)}) custom-call(f32[512,512]{1,0:T(8,128)} %get-tuple-element.22.l_in, f32[512,512]{1,0:T(8,128)} %get-tuple-element.23.m_in), custom_call_target="tpu_custom_call" | custom-call | tf_op jit(solution)/shard_map/factor_second/pallas_call | solution.py:174
  156.5 7.6 %factor_third.1 = (f32[16,512]{1,0:T(8,128)}, bf16[512,512]{1,0:T(8,128)(2,1)}, bf16[512,512]{1,0:T(8,128)(2,1)}) custom-call(s32[1]{0:T(128)} %bitcast.place_ref, f32[512,512]{1,0:T(8,128)} %get-tuple-element.24.l_in, f32[512,512]{1,0:T(8,128)} %get-tuple-element.25.m_in), custom_call_target="tpu_custom_call" | custom-call | tf_op jit(solution)/shard_map/factor_third/pallas_call | solution.py:185
  164.1 4.9 %shard_map.118 = (f32[1024,512]{1,0:T(8,128)}, bf16[1024,512]{1,0:T(8,128)(2,1)}, bf16[1024,512]{1,0:T(8,128)(2,1)}) custom-call(f32[1024,512]{1,0:T(8,128)S(1)} %copy-done, bf16[512,512]{1,0:T(8,128)(2,1)} %get-tuple-element.27.wh.refs_4_.refs_9_, bf16[512,512]{1,0:T(8,128)(2,1)} %get-tuple-element.28.wl.refs_5_.refs_10_), custom_call_target="tpu_custom_call" | custom-call | tf_op jit(solution)/shard_map/pallas_call | solution.py:261
  169.0 19.2 %shard_map.119 = (f32[2048,1024]{1,0:T(8,128)}, bf16[2048,512]{1,0:T(8,128)(2,1)}, bf16[2048,512]{1,0:T(8,128)(2,1)}) custom-call(s32[2]{0:T(128)S(1)} %pad_add_fusion.1.pick_ref, f32[1024,512]{1,0:T(8,128)S(1)} %copy-done.2, f32[1024,512]{1,0:T(8,128)} %collective-permute-done.11.refs_1_, f32[1024,512]{1,0:T(8,128)} %collective-permute-done.12.refs_2_, ...), custom_call_target="tpu_custom_call" | custom-call | tf_op jit(solution)/shard_map/pallas_call | solution.py:321
  188.3 27.2 %shard_map.120 = (f32[2048,2048]{1,0:T(8,128)}, f32[1024,256]{1,0:T(8,128)}, f32[2048,256]{1,0:T(8,128)}) custom-call(s32[3]{0:T(128)S(1)} %pad_add_fusion.2.flag_ref, f32[128,2048]{1,0:T(8,128)S(1)} %copy-done.3, f32[128,2048]{1,0:T(8,128)} %collective-permute-done.14.refs_1_, f32[128,2048]{1,0:T(8,128)} %collective-permute-done.15.refs_2_, ...), custom_call_target="tpu_custom_call" | custom-call | tf_op jit(solution)/shard_map/pallas_call | solution.py:372
  (48 shorter events, 0.4 us)
Async XLA Ops:
  0.6 2.0 collective-permute-start.10
  2.7 55.9 %copy-start.3 = (f32[128,2048]{1,0:T(8,128)S(1)}, f32[128,2048]{1,0:T(8,128)}, u32[]{:S(2)}) copy-start(f32[128,2048]{1,0:T(8,128)} %refs_0_.1) | copy-start | bytes 3145732
  2.7 55.9 %copy-start.12 = (f32[16,512]{1,0:T(8,128)S(1)}, f32[16,512]{1,0:T(8,128)}, u32[]{:S(2)}) copy-start(f32[16,512]{1,0:T(8,128)} %param.7) | copy-start | bytes 98308
  4.8 143.3 %copy-start.1 = (f32[1024,512]{1,0:T(8,128)}, f32[1024,512]{1,0:T(8,128)S(1)}, u32[]{:S(2)}) copy-start(f32[1024,512]{1,0:T(8,128)S(1)} %broadcast_select_fusion.refs_0_) | copy-start | bytes 6291460
  4.8 50.3 %collective-permute-start.12 = (f32[1024,512]{1,0:T(8,128)S(1)}, f32[1024,512]{1,0:T(8,128)}, u32[]{:S(2)}, u32[]{:S(2)}) collective-permute-start(f32[1024,512]{1,0:T(8,128)S(1)} %broadcast_select_fusion.refs_0_), channel_id=1, source_target_pairs={{0,4},{2,6},{10,14},{8,12},{20,16},{22,18},{30,26},{28,24},{1,3},{... | collective-permute-start | bytes 6291464 | tf_op jit(solution)/shard_map/ppermute | solution.py:450
  6.1 124.3 %collective-permute-start.11 = (f32[1024,512]{1,0:T(8,128)S(1)}, f32[1024,512]{1,0:T(8,128)}, u32[]{:S(2)}, u32[]{:S(2)}) collective-permute-start(f32[1024,512]{1,0:T(8,128)S(1)} %broadcast_select_fusion.refs_0_), channel_id=1, source_target_pairs={{0,1},{1,0},{2,3},{3,2},{4,5},{5,4},{6,7},{7,6},{8,9},{9,8},{10,11... | collective-permute-start | bytes 6291464 | tf_op jit(solution)/shard_map/ppermute | solution.py:389
  55.2 75.3 %collective-permute-start.13 = (f32[1024,512]{1,0:T(8,128)}, f32[1024,512]{1,0:T(8,128)}, u32[]{:S(2)}, u32[]{:S(2)}) collective-permute-start(f32[1024,512]{1,0:T(8,128)} %collective-permute-done.12.refs_2_), channel_id=1, source_target_pairs={{0,1},{1,0},{2,3},{3,2},{4,5},{5,4},{6,7},{7,6},{8,9},{9,8},{10,11... | collective-permute-start | bytes 6291464 | tf_op jit(solution)/shard_map/ppermute | solution.py:389
  58.6 69.4 %collective-permute-start.14 = (f32[128,2048]{1,0:T(8,128)S(1)}, f32[128,2048]{1,0:T(8,128)}, u32[]{:S(2)}, u32[]{:S(2)}) collective-permute-start(f32[128,2048]{1,0:T(8,128)S(1)} %copy-done.3), channel_id=1, source_target_pairs={{0,16},{8,24},{16,0},{24,8},{1,17},{9,25},{17,1},{25,9},{2,18},{10... | collective-permute-start | bytes 3145736 | tf_op jit(solution)/shard_map/ppermute | solution.py:389
  58.6 23.7 %collective-permute-start = (f32[16,512]{1,0:T(8,128)S(1)}, f32[16,512]{1,0:T(8,128)S(1)}, u32[]{:S(2)}, u32[]{:S(2)}) collective-permute-start(f32[16,512]{1,0:T(8,128)S(1)} %copy-done.12), channel_id=1, source_target_pairs={{0,8},{8,0},{16,24},{24,16},{1,9},{9,1},{17,25},{25,17},{2,10},{10... | collective-permute-start | bytes 98312 | tf_op jit(solution)/shard_map/ppermute | solution.py:389
  58.6 50.8 %collective-permute-start.2 = (f32[16,512]{1,0:T(8,128)S(1)}, f32[16,512]{1,0:T(8,128)S(1)}, u32[]{:S(2)}, u32[]{:S(2)}) collective-permute-start(f32[16,512]{1,0:T(8,128)S(1)} %copy-done.12), channel_id=1, source_target_pairs={{0,24},{8,16},{16,8},{24,0},{1,25},{9,17},{17,9},{25,1},{2,26},{10... | collective-permute-start | bytes 98312 | tf_op jit(solution)/shard_map/ppermute | solution.py:389
  82.3 27.9 %collective-permute-start.1 = (f32[16,512]{1,0:T(8,128)S(1)}, f32[16,512]{1,0:T(8,128)S(1)}, u32[]{:S(2)}, u32[]{:S(2)}) collective-permute-start(f32[16,512]{1,0:T(8,128)S(1)} %copy-done.12), channel_id=1, source_target_pairs={{0,16},{8,24},{16,0},{24,8},{1,17},{9,25},{17,1},{25,9},{2,18},{10... | collective-permute-start | bytes 98312 | tf_op jit(solution)/shard_map/ppermute | solution.py:389
  109.5 3.8 %collective-permute-start.20 = (f32[128,256]{1,0:T(8,128)S(1)}, f32[128,256]{1,0:T(8,128)S(1)}, u32[]{:S(2)}, u32[]{:S(2)}) collective-permute-start(f32[128,256]{1,0:T(8,128)S(1)} %get-tuple-element.38), channel_id=1, source_target_pairs={{0,24},{8,16},{16,8},{24,0},{1,25},{9,17},{17,9},{25,1},{2,26},{10... | collective-permute-start | bytes 393224 | tf_op jit(solution)/shard_map/ppermute | solution.py:389
  110.2 17.8 %copy-start.4 = (f32[4,16,512]{2,1,0:T(8,128)}, f32[4,16,512]{2,1,0:T(8,128)S(1)}, u32[]{:S(2)}) copy-start(f32[4,16,512]{2,1,0:T(8,128)S(1)} %pad_maximum_fusion.refs_0_) | copy-start | bytes 393220
  110.2 5.2 %collective-permute-start.8 = (f32[4,16,512]{2,1,0:T(8,128)S(1)}, f32[4,16,512]{2,1,0:T(8,128)S(1)}, u32[]{:S(2)}, u32[]{:S(2)}) collective-permute-start(f32[4,16,512]{2,1,0:T(8,128)S(1)} %pad_maximum_fusion.refs_0_), channel_id=1, source_target_pairs={{0,6},{1,7},{2,4},{3,5},{4,2},{5,3},{6,0},{7,1},{8,14},{9,15},{10,... | collective-permute-start | bytes 393224 | tf_op jit(solution)/shard_map/ppermute | solution.py:389
  113.3 4.5 %collective-permute-start.6 = (f32[4,16,512]{2,1,0:T(8,128)S(1)}, f32[4,16,512]{2,1,0:T(8,128)S(1)}, u32[]{:S(2)}, u32[]{:S(2)}) collective-permute-start(f32[4,16,512]{2,1,0:T(8,128)S(1)} %pad_maximum_fusion.refs_0_), channel_id=1, source_target_pairs={{0,4},{1,5},{2,6},{3,7},{4,0},{5,1},{6,2},{7,3},{8,12},{9,13},{10,... | collective-permute-start | bytes 393224 | tf_op jit(solution)/shard_map/ppermute | solution.py:389
  115.4 12.6 %copy-start.5 = (f32[4,16,512]{2,1,0:T(8,128)}, f32[4,16,512]{2,1,0:T(8,128)S(1)}, u32[]{:S(2)}) copy-start(f32[4,16,512]{2,1,0:T(8,128)S(1)} %collective-permute-done.8.refs_6_) | copy-start | bytes 393220
  115.4 5.5 %collective-permute-start.4 = (f32[4,16,512]{2,1,0:T(8,128)S(1)}, f32[4,16,512]{2,1,0:T(8,128)S(1)}, u32[]{:S(2)}, u32[]{:S(2)}) collective-permute-start(f32[4,16,512]{2,1,0:T(8,128)S(1)} %pad_maximum_fusion.refs_0_), channel_id=1, source_target_pairs={{0,2},{1,3},{2,0},{3,1},{4,6},{5,7},{6,4},{7,5},{8,10},{9,11},{10,... | collective-permute-start | bytes 393224 | tf_op jit(solution)/shard_map/ppermute | solution.py:389
  117.8 10.2 %copy-start.6 = (f32[4,16,512]{2,1,0:T(8,128)}, f32[4,16,512]{2,1,0:T(8,128)S(1)}, u32[]{:S(2)}) copy-start(f32[4,16,512]{2,1,0:T(8,128)S(1)} %collective-permute-done.6.refs_4_) | copy-start | bytes 393220
  117.8 4.3 %collective-permute-start.3 = (f32[4,16,512]{2,1,0:T(8,128)S(1)}, f32[4,16,512]{2,1,0:T(8,128)S(1)}, u32[]{:S(2)}, u32[]{:S(2)}) collective-permute-start(f32[4,16,512]{2,1,0:T(8,128)S(1)} %pad_maximum_fusion.refs_0_), channel_id=1, source_target_pairs={{0,1},{1,0},{2,3},{3,2},{4,5},{5,4},{6,7},{7,6},{8,9},{9,8},{10,11... | collective-permute-start | bytes 393224 | tf_op jit(solution)/shard_map/ppermute | solution.py:389
  120.9 7.1 %copy-start.7 = (f32[4,16,512]{2,1,0:T(8,128)}, f32[4,16,512]{2,1,0:T(8,128)S(1)}, u32[]{:S(2)}) copy-start(f32[4,16,512]{2,1,0:T(8,128)S(1)} %collective-permute-done.4.refs_2_) | copy-start | bytes 393220
  120.9 2.2 %collective-permute-start.9 = (f32[4,16,512]{2,1,0:T(8,128)S(1)}, f32[4,16,512]{2,1,0:T(8,128)S(1)}, u32[]{:S(2)}, u32[]{:S(2)}) collective-permute-start(f32[4,16,512]{2,1,0:T(8,128)S(1)} %collective-permute-done.8.refs_6_), channel_id=1, source_target_pairs={{0,1},{1,0},{2,3},{3,2},{4,5},{5,4},{6,7},{7,6},{8,9},{9,8},{10,11... | collective-permute-start | bytes 393224 | tf_op jit(solution)/shard_map/ppermute | solution.py:389
  122.1 5.9 %copy-start.8 = (f32[4,16,512]{2,1,0:T(8,128)}, f32[4,16,512]{2,1,0:T(8,128)S(1)}, u32[]{:S(2)}) copy-start(f32[4,16,512]{2,1,0:T(8,128)S(1)} %collective-permute-done.3.refs_1_) | copy-start | bytes 393220
  122.1 1.3 collective-permute-start.7
  123.1 4.9 %copy-start.9 = (f32[4,16,512]{2,1,0:T(8,128)}, f32[4,16,512]{2,1,0:T(8,128)S(1)}, u32[]{:S(2)}) copy-start(f32[4,16,512]{2,1,0:T(8,128)S(1)} %collective-permute-done.9.refs_7_) | copy-start | bytes 393220
  123.1 1.7 collective-permute-start.5
  123.5 64.8 %collective-permute-start.15 = (f32[128,2048]{1,0:T(8,128)S(1)}, f32[128,2048]{1,0:T(8,128)}, u32[]{:S(2)}, u32[]{:S(2)}) collective-permute-start(f32[128,2048]{1,0:T(8,128)S(1)} %copy-done.3), channel_id=1, source_target_pairs={{0,8},{8,0},{16,24},{24,16},{1,9},{9,1},{17,25},{25,17},{2,10},{10... | collective-permute-start | bytes 3145736 | tf_op jit(solution)/shard_map/ppermute | solution.py:389
  124.8 63.5 %collective-permute-start.16 = (f32[128,2048]{1,0:T(8,128)S(1)}, f32[128,2048]{1,0:T(8,128)}, u32[]{:S(2)}, u32[]{:S(2)}) collective-permute-start(f32[128,2048]{1,0:T(8,128)S(1)} %copy-done.3), channel_id=1, source_target_pairs={{8,16},{16,8},{9,17},{17,9},{10,18},{18,10},{11,19},{19,11},{12,20... | collective-permute-start | bytes 3145736 | tf_op jit(solution)/shard_map/ppermute | solution.py:426
  128.1 60.2 %collective-permute-start.17 = (f32[128,2048]{1,0:T(8,128)}, f32[128,2048]{1,0:T(8,128)}, u32[]{:S(2)}, u32[]{:S(2)}) collective-permute-start(f32[128,2048]{1,0:T(8,128)} %collective-permute-done.14.refs_1_), channel_id=1, source_target_pairs={{8,0},{16,24},{9,1},{17,25},{10,2},{18,26},{11,3},{19,27},{12,4},{... | collective-permute-start | bytes 3145736 | tf_op jit(solution)/shard_map/ppermute | solution.py:476
  130.5 57.8 %collective-permute-start.18 = (f32[128,256]{1,0:T(8,128)}, f32[128,256]{1,0:T(8,128)S(1)}, u32[]{:S(2)}, u32[]{:S(2)}) collective-permute-start(f32[128,256]{1,0:T(8,128)} %get-tuple-element.39), channel_id=1, source_target_pairs={{0,16},{8,24},{16,0},{24,8},{1,17},{9,25},{17,1},{25,9},{2,18},{10... | collective-permute-start | bytes 393224 | tf_op jit(solution)/shard_map/ppermute | solution.py:389
  130.5 57.8 %collective-permute-start.19 = (f32[128,256]{1,0:T(8,128)}, f32[128,256]{1,0:T(8,128)}, u32[]{:S(2)}, u32[]{:S(2)}) collective-permute-start(f32[128,256]{1,0:T(8,128)} %get-tuple-element.41), channel_id=1, source_target_pairs={{0,8},{8,0},{16,24},{24,16},{1,9},{9,1},{17,25},{25,17},{2,10},{10... | collective-permute-start | bytes 393224 | tf_op jit(solution)/shard_map/ppermute | solution.py:389
  148.1 16.0 %copy-start = (f32[1024,512]{1,0:T(8,128)S(1)}, f32[1024,512]{1,0:T(8,128)}, u32[]{:S(2)}) copy-start(f32[1024,512]{1,0:T(8,128)} %c_ref.1) | copy-start | bytes 6291460
  164.1 4.9 %copy-start.2 = (f32[1024,512]{1,0:T(8,128)S(1)}, f32[1024,512]{1,0:T(8,128)}, u32[]{:S(2)}) copy-start(f32[1024,512]{1,0:T(8,128)} %copy-done.1) | copy-start | bytes 6291460
  (2 other events, 7.9 us)

commit v2 on v1

--- a/solution.py
+++ b/solution.py
@@ -300,33 +300,47 @@
     total, width = trail.shape
     steps = count // tile
 
+    n = len(crosses)
+
     def kernel(pick_ref, *refs):
-        choices, (wh, wl, oh, ol, t_ref, out_ref, ch_ref, cl_ref) = (
-            refs[: len(crosses)],
-            refs[len(crosses) :],
-        )
-        pick = pick_ref[pl.program_id(0) // steps]
-        x = choices[0][...]
-        for i in range(1, len(choices)):
-            x = jnp.where(pick == i, choices[i][...], x)
+        choices, refs = refs[:n], refs[n:]
+        wh, wl, oh, ol, t_ref, out_ref, ch_ref, cl_ref, x_ref, sems = refs
+        i = pl.program_id(0)
+
+        def take(k, source, j, target):
+            return pltpu.make_async_copy(
+                choices[k].at[pl.ds(source, tile)], x_ref.at[pl.ds(target, tile)], sems.at[j]
+            )
+
+        @pl.when(i == 0)
+        def _():
+            for j in range(total // tile):
+                for k in range(n):
+
+                    @pl.when(pick_ref[j // steps] == k)
+                    def _():
+                        take(k, (j % steps) * tile, j, j * tile).start()
+
+        place = pl.multiple_of(i * tile, tile)
+        take(0, 0, i, place).wait()
+        x = x_ref[pl.ds(place, tile), :]
         r = split(lower_nt(split(x), (wh, wl)))
         out_ref[...] = t_ref[...] - product(r, (oh[...], ol[...]), NT)
         ch_ref[...], cl_ref[...] = split(lower_nn(r, (wh, wl)))
 
-    def side(which):
-        return pl.BlockSpec(
-            (tile, pw), lambda i, p: (jnp.where(p[i // steps] == which, i % steps, 0), 0)
-        )
-
     return run(
         kernel,
         total // tile,
-        [side(k) for k in range(len(crosses))]
+        [pl.BlockSpec(memory_space=pl.ANY)] * n
         + [full(pw, pw)] * 2
         + [full(*own[0].shape)] * 2
         + [tiles(tile, width)],
         (tiles(tile, width), tiles(tile, pw), tiles(tile, pw)),
         (shape(total, width),) + (pltpu.HBM((total, pw), jnp.bfloat16),) * 2,
+        scratch=[
+            pltpu.VMEM((total, pw), jnp.float32),
+            pltpu.SemaphoreType.DMA((total // tile,)),
+        ],
         prefetch=1,
     )(picks, *crosses, *inverse, *own, trail)
 

time: 219 us -> 219 us (level)
  transfers between devices with their start and end apart: 21 -> 21, of which waited for: 7 -> 7; matrix products, arithmetic and copies ran while one was open for 1% -> 1% of each run, Pallas kernels for 25% -> 26%
where the time goes in v2:
time: 219 us; the launch traced here: 216 us
  waiting for transfers between devices  99.8 us (46%)
  Pallas kernels  82.3 us (38%)
  starting transfers between devices  27.8 us (13%)
  other arithmetic  2.99 us (1%)
    ppermute x17, waiting for transfers between devices, exchange(): return lax.ppermute(x, axis, [(i, i ^ mask) for i in range(size)])  51.5 us
    ppermute x2, waiting for transfers between devices, update(): got = lax.ppermute(held, ('row', 'col'), pairs)  48.3 us
    pallas_call x1, Pallas kernels, maps(): run(kernel, steps, [full(*x.shape) for x in arrays + list(sectors)] + [fu...  27.2 us
    pallas_call x1, Pallas kernels, rows(): run(kernel, total // tile, [pl.BlockSpec(memory_space=pl.ANY)] * n + [ful...  19.3 us
    ppermute x17, starting transfers between devices, exchange(): return lax.ppermute(x, axis, [(i, i ^ mask) for i in range(size)])  18.9 us
    pallas_call x1, Pallas kernels, first(): pl.pallas_call(first_kernel, out_shape=(square, square), in_specs=[smem]...  14.9 us
    pallas_call x1, Pallas kernels, second(): pl.pallas_call(second_kernel, out_shape=(square, square), in_specs=[vmem,...  8.38 us
    pallas_call x1, Pallas kernels, third(): pl.pallas_call(third_kernel, out_shape=results, in_specs=[smem, vmem, vme...  7.56 us
  transfers between devices with their start and end apart: 21, of which 7 were waited for; matrix products, arithmetic and copies ran while one was open for 1% of the time, Pallas kernels for 26%

profile of v2, /device:TPU:19, one launch (start us, length us, event | category | flops | bytes accessed | tf_op | source)
XLA Modules:
  0.0 215.8 jit_solution(5691245494715528883)
XLA Ops:
  0.6 2.0 collective-permute-start.10
  2.7 2.2 %broadcast_select_fusion.refs_0_ = f32[1024,512]{1,0:T(8,128)S(1)} fusion(f32[1024,512]{1,0:T(8,128)} %collective-permute-done.10, f32[1024,512]{1,0:T(8,128)} %c_ref.1, pred[]{:T(512)S(6)} %or.18), kind=kLoop, calls=%fused_computation | loop fusion | flops 524288 | bytes 6291457 | tf_op jit(solution)/shard_map/jit(_where)/select_n | solution.py:467
  4.8 1.3 collective-permute-start.12
  6.1 0.7 collective-permute-start.11
  6.9 48.3 %collective-permute-done.12.refs_2_ = f32[1024,512]{1,0:T(8,128)} collective-permute-done((f32[1024,512]{1,0:T(8,128)S(1)}, f32[1024,512]{1,0:T(8,128)}, u32[]{:S(2)}, u32[]{:S(2)}) %collective-permute-start.12) | collective-permute-done | bytes 2097184 | tf_op jit(solution)/shard_map/ppermute | solution.py:464
  55.2 3.4 %collective-permute-start.13 = (f32[1024,512]{1,0:T(8,128)}, f32[1024,512]{1,0:T(8,128)}, u32[]{:S(2)}, u32[]{:S(2)}) collective-permute-start(f32[1024,512]{1,0:T(8,128)} %collective-permute-done.12.refs_2_), channel_id=1, source_target_pairs={{0,1},{1,0},{2,3},{3,2},{4,5},{5,4},{6,7},{7,6},{8,9},{9,8},{10,11... | collective-permute-start | bytes 6291464 | tf_op jit(solution)/shard_map/ppermute | solution.py:403
  58.6 2.6 %collective-permute-start.2 = (f32[16,512]{1,0:T(8,128)S(1)}, f32[16,512]{1,0:T(8,128)S(1)}, u32[]{:S(2)}, u32[]{:S(2)}) collective-permute-start(f32[16,512]{1,0:T(8,128)S(1)} %copy-done.12), channel_id=1, source_target_pairs={{0,24},{8,16},{16,8},{24,0},{1,25},{9,17},{17,9},{25,1},{2,26},{10... | collective-permute-start | bytes 98312 | tf_op jit(solution)/shard_map/ppermute | solution.py:403
  61.2 21.1 %collective-permute-done = f32[16,512]{1,0:T(8,128)S(1)} collective-permute-done((f32[16,512]{1,0:T(8,128)S(1)}, f32[16,512]{1,0:T(8,128)S(1)}, u32[]{:S(2)}, u32[]{:S(2)}) %collective-permute-start) | collective-permute-done | bytes 32800 | tf_op jit(solution)/shard_map/ppermute | solution.py:403
  82.3 1.9 collective-permute-start.1
  84.2 1.8 constant_dynamic-slice_fusion
  86.0 23.5 %collective-permute-done.2 = f32[16,512]{1,0:T(8,128)S(1)} collective-permute-done((f32[16,512]{1,0:T(8,128)S(1)}, f32[16,512]{1,0:T(8,128)S(1)}, u32[]{:S(2)}, u32[]{:S(2)}) %collective-permute-start.2) | collective-permute-done | bytes 32800 | tf_op jit(solution)/shard_map/ppermute | solution.py:403
  109.5 0.7 collective-permute-start.20
  110.3 3.0 %collective-permute-done.20.refs_8_ = f32[128,256]{1,0:T(8,128)S(1)} collective-permute-done((f32[128,256]{1,0:T(8,128)S(1)}, f32[128,256]{1,0:T(8,128)S(1)}, u32[]{:S(2)}, u32[]{:S(2)}) %collective-permute-start.20) | collective-permute-done | bytes 131104 | tf_op jit(solution)/shard_map/ppermute | solution.py:403
  113.3 2.1 collective-permute-done.8.refs_6_
  115.4 1.4 collective-permute-start.4
  116.8 1.0 collective-permute-done.6.refs_4_
  117.8 3.1 %collective-permute-start.3 = (f32[4,16,512]{2,1,0:T(8,128)S(1)}, f32[4,16,512]{2,1,0:T(8,128)S(1)}, u32[]{:S(2)}, u32[]{:S(2)}) collective-permute-start(f32[4,16,512]{2,1,0:T(8,128)S(1)} %pad_maximum_fusion.refs_0_), channel_id=1, source_target_pairs={{0,1},{1,0},{2,3},{3,2},{4,5},{5,4},{6,7},{7,6},{8,9},{9,8},{10,11... | collective-permute-start | bytes 393224 | tf_op jit(solution)/shard_map/ppermute | solution.py:403
  120.9 1.2 collective-permute-start.9
  122.1 0.1 collective-permute-start.7
  122.3 0.8 collective-permute-done.9.refs_7_
  123.1 0.4 collective-permute-start.5
  123.5 1.3 collective-permute-start.15
  124.8 3.2 %collective-permute-start.16 = (f32[128,2048]{1,0:T(8,128)S(1)}, f32[128,2048]{1,0:T(8,128)}, u32[]{:S(2)}, u32[]{:S(2)}) collective-permute-start(f32[128,2048]{1,0:T(8,128)S(1)} %copy-done.3), channel_id=1, source_target_pairs={{8,16},{16,8},{9,17},{17,9},{10,18},{18,10},{11,19},{19,11},{12,20... | collective-permute-start | bytes 3145736 | tf_op jit(solution)/shard_map/ppermute | solution.py:440
  128.1 2.3 %collective-permute-start.17 = (f32[128,2048]{1,0:T(8,128)}, f32[128,2048]{1,0:T(8,128)}, u32[]{:S(2)}, u32[]{:S(2)}) collective-permute-start(f32[128,2048]{1,0:T(8,128)} %collective-permute-done.14.refs_1_), channel_id=1, source_target_pairs={{8,0},{16,24},{9,1},{17,25},{10,2},{18,26},{11,3},{19,27},{12,4},{... | collective-permute-start | bytes 3145736 | tf_op jit(solution)/shard_map/ppermute | solution.py:490
  130.5 2.0 collective-permute-start.19
  132.5 0.7 pad_add_fusion.place_ref
  133.2 14.9 %factor_first.1 = (f32[512,512]{1,0:T(8,128)}, f32[512,512]{1,0:T(8,128)}) custom-call(s32[2]{0:T(128)} %pad_add_fusion.place_ref, f32[4,16,512]{2,1,0:T(8,128)} %copy-done.4, f32[4,16,512]{2,1,0:T(8,128)} %copy-done.8, f32[4,16,512]{2,1,0:T(8,128)} %copy-done.7, f32[4,16,512]{2,1,0:T(8,128)} %copy-done.11, f32[4,16,512]{2,1,0:T(8,128)} %copy-done.6, ...), custom_call_target="tpu_custom_call" | custom-call | tf_op jit(solution)/shard_map/factor_first/pallas_call | solution.py:164
  148.1 8.4 %factor_second.1 = (f32[512,512]{1,0:T(8,128)}, f32[512,512]{1,0:T(8,128)}) custom-call(f32[512,512]{1,0:T(8,128)} %get-tuple-element.22.l_in, f32[512,512]{1,0:T(8,128)} %get-tuple-element.23.m_in), custom_call_target="tpu_custom_call" | custom-call | tf_op jit(solution)/shard_map/factor_second/pallas_call | solution.py:174
  156.5 7.6 %factor_third.1 = (f32[16,512]{1,0:T(8,128)}, bf16[512,512]{1,0:T(8,128)(2,1)}, bf16[512,512]{1,0:T(8,128)(2,1)}) custom-call(s32[1]{0:T(128)} %bitcast.place_ref, f32[512,512]{1,0:T(8,128)} %get-tuple-element.24.l_in, f32[512,512]{1,0:T(8,128)} %get-tuple-element.25.m_in), custom_call_target="tpu_custom_call" | custom-call | tf_op jit(solution)/shard_map/factor_third/pallas_call | solution.py:185
  164.1 4.9 %shard_map.118 = (f32[1024,512]{1,0:T(8,128)}, bf16[1024,512]{1,0:T(8,128)(2,1)}, bf16[1024,512]{1,0:T(8,128)(2,1)}) custom-call(f32[1024,512]{1,0:T(8,128)S(1)} %copy-done, bf16[512,512]{1,0:T(8,128)(2,1)} %get-tuple-element.27.wh.refs_4_.refs_9_, bf16[512,512]{1,0:T(8,128)(2,1)} %get-tuple-element.28.wl.refs_5_.refs_10_), custom_call_target="tpu_custom_call" | custom-call | tf_op jit(solution)/shard_map/pallas_call | solution.py:261
  169.0 19.3 %shard_map.119 = (f32[2048,1024]{1,0:T(8,128)}, bf16[2048,512]{1,0:T(8,128)(2,1)}, bf16[2048,512]{1,0:T(8,128)(2,1)}) custom-call(s32[2]{0:T(128)S(1)} %pad_add_fusion.1.pick_ref, f32[1024,512]{1,0:T(8,128)S(1)} %copy-done.2, f32[1024,512]{1,0:T(8,128)} %collective-permute-done.11.refs_1_, f32[1024,512]{1,0:T(8,128)} %collective-permute-done.12.refs_2_, ...), custom_call_target="tpu_custom_call" | custom-call | tf_op jit(solution)/shard_map/pallas_call | solution.py:331
  188.4 27.2 %shard_map.120 = (f32[2048,2048]{1,0:T(8,128)}, f32[1024,256]{1,0:T(8,128)}, f32[2048,256]{1,0:T(8,128)}) custom-call(s32[3]{0:T(128)S(1)} %pad_add_fusion.2.flag_ref, f32[128,2048]{1,0:T(8,128)S(1)} %copy-done.3, f32[128,2048]{1,0:T(8,128)} %collective-permute-done.14.refs_1_, f32[128,2048]{1,0:T(8,128)} %collective-permute-done.15.refs_2_, ...), custom_call_target="tpu_custom_call" | custom-call | tf_op jit(solution)/shard_map/pallas_call | solution.py:386
  (48 shorter events, 0.4 us)
Async XLA Ops:
  0.6 2.0 collective-permute-start.10
  2.7 55.9 %copy-start.3 = (f32[128,2048]{1,0:T(8,128)S(1)}, f32[128,2048]{1,0:T(8,128)}, u32[]{:S(2)}) copy-start(f32[128,2048]{1,0:T(8,128)} %refs_0_.1) | copy-start | bytes 3145732
  2.7 55.9 %copy-start.12 = (f32[16,512]{1,0:T(8,128)S(1)}, f32[16,512]{1,0:T(8,128)}, u32[]{:S(2)}) copy-start(f32[16,512]{1,0:T(8,128)} %param.7) | copy-start | bytes 98308
  4.8 143.3 %copy-start.1 = (f32[1024,512]{1,0:T(8,128)}, f32[1024,512]{1,0:T(8,128)S(1)}, u32[]{:S(2)}) copy-start(f32[1024,512]{1,0:T(8,128)S(1)} %broadcast_select_fusion.refs_0_) | copy-start | bytes 6291460
  4.8 50.3 %collective-permute-start.12 = (f32[1024,512]{1,0:T(8,128)S(1)}, f32[1024,512]{1,0:T(8,128)}, u32[]{:S(2)}, u32[]{:S(2)}) collective-permute-start(f32[1024,512]{1,0:T(8,128)S(1)} %broadcast_select_fusion.refs_0_), channel_id=1, source_target_pairs={{0,4},{2,6},{10,14},{8,12},{20,16},{22,18},{30,26},{28,24},{1,3},{... | collective-permute-start | bytes 6291464 | tf_op jit(solution)/shard_map/ppermute | solution.py:464
  6.1 124.3 %collective-permute-start.11 = (f32[1024,512]{1,0:T(8,128)S(1)}, f32[1024,512]{1,0:T(8,128)}, u32[]{:S(2)}, u32[]{:S(2)}) collective-permute-start(f32[1024,512]{1,0:T(8,128)S(1)} %broadcast_select_fusion.refs_0_), channel_id=1, source_target_pairs={{0,1},{1,0},{2,3},{3,2},{4,5},{5,4},{6,7},{7,6},{8,9},{9,8},{10,11... | collective-permute-start | bytes 6291464 | tf_op jit(solution)/shard_map/ppermute | solution.py:403
  55.2 75.3 %collective-permute-start.13 = (f32[1024,512]{1,0:T(8,128)}, f32[1024,512]{1,0:T(8,128)}, u32[]{:S(2)}, u32[]{:S(2)}) collective-permute-start(f32[1024,512]{1,0:T(8,128)} %collective-permute-done.12.refs_2_), channel_id=1, source_target_pairs={{0,1},{1,0},{2,3},{3,2},{4,5},{5,4},{6,7},{7,6},{8,9},{9,8},{10,11... | collective-permute-start | bytes 6291464 | tf_op jit(solution)/shard_map/ppermute | solution.py:403
  58.6 69.4 %collective-permute-start.14 = (f32[128,2048]{1,0:T(8,128)S(1)}, f32[128,2048]{1,0:T(8,128)}, u32[]{:S(2)}, u32[]{:S(2)}) collective-permute-start(f32[128,2048]{1,0:T(8,128)S(1)} %copy-done.3), channel_id=1, source_target_pairs={{0,16},{8,24},{16,0},{24,8},{1,17},{9,25},{17,1},{25,9},{2,18},{10... | collective-permute-start | bytes 3145736 | tf_op jit(solution)/shard_map/ppermute | solution.py:403
  58.6 23.7 %collective-permute-start = (f32[16,512]{1,0:T(8,128)S(1)}, f32[16,512]{1,0:T(8,128)S(1)}, u32[]{:S(2)}, u32[]{:S(2)}) collective-permute-start(f32[16,512]{1,0:T(8,128)S(1)} %copy-done.12), channel_id=1, source_target_pairs={{0,8},{8,0},{16,24},{24,16},{1,9},{9,1},{17,25},{25,17},{2,10},{10... | collective-permute-start | bytes 98312 | tf_op jit(solution)/shard_map/ppermute | solution.py:403
  58.6 50.8 %collective-permute-start.2 = (f32[16,512]{1,0:T(8,128)S(1)}, f32[16,512]{1,0:T(8,128)S(1)}, u32[]{:S(2)}, u32[]{:S(2)}) collective-permute-start(f32[16,512]{1,0:T(8,128)S(1)} %copy-done.12), channel_id=1, source_target_pairs={{0,24},{8,16},{16,8},{24,0},{1,25},{9,17},{17,9},{25,1},{2,26},{10... | collective-permute-start | bytes 98312 | tf_op jit(solution)/shard_map/ppermute | solution.py:403
  82.3 27.9 %collective-permute-start.1 = (f32[16,512]{1,0:T(8,128)S(1)}, f32[16,512]{1,0:T(8,128)S(1)}, u32[]{:S(2)}, u32[]{:S(2)}) collective-permute-start(f32[16,512]{1,0:T(8,128)S(1)} %copy-done.12), channel_id=1, source_target_pairs={{0,16},{8,24},{16,0},{24,8},{1,17},{9,25},{17,1},{25,9},{2,18},{10... | collective-permute-start | bytes 98312 | tf_op jit(solution)/shard_map/ppermute | solution.py:403
  109.5 3.8 %collective-permute-start.20 = (f32[128,256]{1,0:T(8,128)S(1)}, f32[128,256]{1,0:T(8,128)S(1)}, u32[]{:S(2)}, u32[]{:S(2)}) collective-permute-start(f32[128,256]{1,0:T(8,128)S(1)} %get-tuple-element.38), channel_id=1, source_target_pairs={{0,24},{8,16},{16,8},{24,0},{1,25},{9,17},{17,9},{25,1},{2,26},{10... | collective-permute-start | bytes 393224 | tf_op jit(solution)/shard_map/ppermute | solution.py:403
  110.2 17.8 %copy-start.4 = (f32[4,16,512]{2,1,0:T(8,128)}, f32[4,16,512]{2,1,0:T(8,128)S(1)}, u32[]{:S(2)}) copy-start(f32[4,16,512]{2,1,0:T(8,128)S(1)} %pad_maximum_fusion.refs_0_) | copy-start | bytes 393220
  110.2 5.2 %collective-permute-start.8 = (f32[4,16,512]{2,1,0:T(8,128)S(1)}, f32[4,16,512]{2,1,0:T(8,128)S(1)}, u32[]{:S(2)}, u32[]{:S(2)}) collective-permute-start(f32[4,16,512]{2,1,0:T(8,128)S(1)} %pad_maximum_fusion.refs_0_), channel_id=1, source_target_pairs={{0,6},{1,7},{2,4},{3,5},{4,2},{5,3},{6,0},{7,1},{8,14},{9,15},{10,... | collective-permute-start | bytes 393224 | tf_op jit(solution)/shard_map/ppermute | solution.py:403
  113.3 4.5 %collective-permute-start.6 = (f32[4,16,512]{2,1,0:T(8,128)S(1)}, f32[4,16,512]{2,1,0:T(8,128)S(1)}, u32[]{:S(2)}, u32[]{:S(2)}) collective-permute-start(f32[4,16,512]{2,1,0:T(8,128)S(1)} %pad_maximum_fusion.refs_0_), channel_id=1, source_target_pairs={{0,4},{1,5},{2,6},{3,7},{4,0},{5,1},{6,2},{7,3},{8,12},{9,13},{10,... | collective-permute-start | bytes 393224 | tf_op jit(solution)/shard_map/ppermute | solution.py:403
  115.4 12.6 %copy-start.5 = (f32[4,16,512]{2,1,0:T(8,128)}, f32[4,16,512]{2,1,0:T(8,128)S(1)}, u32[]{:S(2)}) copy-start(f32[4,16,512]{2,1,0:T(8,128)S(1)} %collective-permute-done.8.refs_6_) | copy-start | bytes 393220
  115.4 5.5 %collective-permute-start.4 = (f32[4,16,512]{2,1,0:T(8,128)S(1)}, f32[4,16,512]{2,1,0:T(8,128)S(1)}, u32[]{:S(2)}, u32[]{:S(2)}) collective-permute-start(f32[4,16,512]{2,1,0:T(8,128)S(1)} %pad_maximum_fusion.refs_0_), channel_id=1, source_target_pairs={{0,2},{1,3},{2,0},{3,1},{4,6},{5,7},{6,4},{7,5},{8,10},{9,11},{10,... | collective-permute-start | bytes 393224 | tf_op jit(solution)/shard_map/ppermute | solution.py:403
  117.8 10.2 %copy-start.6 = (f32[4,16,512]{2,1,0:T(8,128)}, f32[4,16,512]{2,1,0:T(8,128)S(1)}, u32[]{:S(2)}) copy-start(f32[4,16,512]{2,1,0:T(8,128)S(1)} %collective-permute-done.6.refs_4_) | copy-start | bytes 393220
  117.8 4.3 %collective-permute-start.3 = (f32[4,16,512]{2,1,0:T(8,128)S(1)}, f32[4,16,512]{2,1,0:T(8,128)S(1)}, u32[]{:S(2)}, u32[]{:S(2)}) collective-permute-start(f32[4,16,512]{2,1,0:T(8,128)S(1)} %pad_maximum_fusion.refs_0_), channel_id=1, source_target_pairs={{0,1},{1,0},{2,3},{3,2},{4,5},{5,4},{6,7},{7,6},{8,9},{9,8},{10,11... | collective-permute-start | bytes 393224 | tf_op jit(solution)/shard_map/ppermute | solution.py:403
  120.9 7.1 %copy-start.7 = (f32[4,16,512]{2,1,0:T(8,128)}, f32[4,16,512]{2,1,0:T(8,128)S(1)}, u32[]{:S(2)}) copy-start(f32[4,16,512]{2,1,0:T(8,128)S(1)} %collective-permute-done.4.refs_2_) | copy-start | bytes 393220
  120.9 2.2 %collective-permute-start.9 = (f32[4,16,512]{2,1,0:T(8,128)S(1)}, f32[4,16,512]{2,1,0:T(8,128)S(1)}, u32[]{:S(2)}, u32[]{:S(2)}) collective-permute-start(f32[4,16,512]{2,1,0:T(8,128)S(1)} %collective-permute-done.8.refs_6_), channel_id=1, source_target_pairs={{0,1},{1,0},{2,3},{3,2},{4,5},{5,4},{6,7},{7,6},{8,9},{9,8},{10,11... | collective-permute-start | bytes 393224 | tf_op jit(solution)/shard_map/ppermute | solution.py:403
  122.1 5.9 %copy-start.8 = (f32[4,16,512]{2,1,0:T(8,128)}, f32[4,16,512]{2,1,0:T(8,128)S(1)}, u32[]{:S(2)}) copy-start(f32[4,16,512]{2,1,0:T(8,128)S(1)} %collective-permute-done.3.refs_1_) | copy-start | bytes 393220
  122.1 1.3 collective-permute-start.7
  123.1 4.9 %copy-start.9 = (f32[4,16,512]{2,1,0:T(8,128)}, f32[4,16,512]{2,1,0:T(8,128)S(1)}, u32[]{:S(2)}) copy-start(f32[4,16,512]{2,1,0:T(8,128)S(1)} %collective-permute-done.9.refs_7_) | copy-start | bytes 393220
  123.1 1.7 collective-permute-start.5
  123.5 64.9 %collective-permute-start.15 = (f32[128,2048]{1,0:T(8,128)S(1)}, f32[128,2048]{1,0:T(8,128)}, u32[]{:S(2)}, u32[]{:S(2)}) collective-permute-start(f32[128,2048]{1,0:T(8,128)S(1)} %copy-done.3), channel_id=1, source_target_pairs={{0,8},{8,0},{16,24},{24,16},{1,9},{9,1},{17,25},{25,17},{2,10},{10... | collective-permute-start | bytes 3145736 | tf_op jit(solution)/shard_map/ppermute | solution.py:403
  124.8 63.6 %collective-permute-start.16 = (f32[128,2048]{1,0:T(8,128)S(1)}, f32[128,2048]{1,0:T(8,128)}, u32[]{:S(2)}, u32[]{:S(2)}) collective-permute-start(f32[128,2048]{1,0:T(8,128)S(1)} %copy-done.3), channel_id=1, source_target_pairs={{8,16},{16,8},{9,17},{17,9},{10,18},{18,10},{11,19},{19,11},{12,20... | collective-permute-start | bytes 3145736 | tf_op jit(solution)/shard_map/ppermute | solution.py:440
  128.1 60.3 %collective-permute-start.17 = (f32[128,2048]{1,0:T(8,128)}, f32[128,2048]{1,0:T(8,128)}, u32[]{:S(2)}, u32[]{:S(2)}) collective-permute-start(f32[128,2048]{1,0:T(8,128)} %collective-permute-done.14.refs_1_), channel_id=1, source_target_pairs={{8,0},{16,24},{9,1},{17,25},{10,2},{18,26},{11,3},{19,27},{12,4},{... | collective-permute-start | bytes 3145736 | tf_op jit(solution)/shard_map/ppermute | solution.py:490
  130.5 57.9 %collective-permute-start.18 = (f32[128,256]{1,0:T(8,128)}, f32[128,256]{1,0:T(8,128)S(1)}, u32[]{:S(2)}, u32[]{:S(2)}) collective-permute-start(f32[128,256]{1,0:T(8,128)} %get-tuple-element.39), channel_id=1, source_target_pairs={{0,16},{8,24},{16,0},{24,8},{1,17},{9,25},{17,1},{25,9},{2,18},{10... | collective-permute-start | bytes 393224 | tf_op jit(solution)/shard_map/ppermute | solution.py:403
  130.5 57.9 %collective-permute-start.19 = (f32[128,256]{1,0:T(8,128)}, f32[128,256]{1,0:T(8,128)}, u32[]{:S(2)}, u32[]{:S(2)}) collective-permute-start(f32[128,256]{1,0:T(8,128)} %get-tuple-element.41), channel_id=1, source_target_pairs={{0,8},{8,0},{16,24},{24,16},{1,9},{9,1},{17,25},{25,17},{2,10},{10... | collective-permute-start | bytes 393224 | tf_op jit(solution)/shard_map/ppermute | solution.py:403
  148.1 16.0 %copy-start = (f32[1024,512]{1,0:T(8,128)S(1)}, f32[1024,512]{1,0:T(8,128)}, u32[]{:S(2)}) copy-start(f32[1024,512]{1,0:T(8,128)} %c_ref.1) | copy-start | bytes 6291460
  164.1 4.9 %copy-start.2 = (f32[1024,512]{1,0:T(8,128)S(1)}, f32[1024,512]{1,0:T(8,128)}, u32[]{:S(2)}) copy-start(f32[1024,512]{1,0:T(8,128)} %copy-done.1) | copy-start | bytes 6291460
  (2 other events, 7.9 us)
